TPU v7x, 512 devices: a whole 4x4x16 slice. The times are simulated.
512 devices in a mesh: ctx: 128 (over z, y, core), tp: 4 (over x).
Axes of the slice: x: 4, y: 4, z: 16, core: 2. Of those that a mesh axis runs over, the one named last changes fastest.
Arguments:
- short_query: bfloat16 [16384, 2048], P('ctx', 'tp'), may hold values from -6 to 6
- short_key: bfloat16 [16384, 2048], P('ctx', 'tp'), may hold values from -6 to 6
- short_value: bfloat16 [16384, 2048], P('ctx', 'tp'), may hold values from -6 to 6
- short_filter: bfloat16 [128, 2048], P(None, 'tp'), may hold values from -0.5 to 0.5
- long_query: bfloat16 [16384, 2048], P('ctx', 'tp'), may hold values from -6 to 6
- long_key: bfloat16 [16384, 2048], P('ctx', 'tp'), may hold values from -6 to 6
- long_filter: bfloat16 [16384, 2048], P('ctx', 'tp'), may hold values from -0.046875 to 0.046875
- out_weight: bfloat16 [2048, 2048], P('tp'), may hold values from -0.125 to 0.125
- out_grad: bfloat16 [16384, 2048], P('ctx', 'tp'), may hold values from -6 to 6
Outputs:
- short_query_grad: bfloat16 [16384, 2048], P('ctx', 'tp')
- short_key_grad: bfloat16 [16384, 2048], P('ctx', 'tp')
- short_value_grad: bfloat16 [16384, 2048], P('ctx', 'tp')
- short_filter_grad: bfloat16 [128, 2048], P(None, 'tp')
- long_query_grad: bfloat16 [16384, 2048], P('ctx', 'tp')
- long_key_grad: bfloat16 [16384, 2048], P('ctx', 'tp')
- long_filter_grad: bfloat16 [16384, 2048], P('ctx', 'tp')
All inputs are finite; a program needn't handle non-finite values.
Results may differ from a plain program's by a relative error of at most 0.015.
Values may be sent and summed in bfloat16 or wider, within the bound.
No kernel may reach another device: no remote copies, remote signals or barrier semaphores. Data moves between devices by JAX's collectives and lax.ppermute only.
A program may use at most 64 MiB of HBM per device.

v0:
```python
import math

import jax
import jax.numpy as jnp
import numpy as np
from jax import lax
from jax.experimental import pallas as pl
from jax.experimental.pallas import tpu as pltpu
from jax.sharding import Mesh
from jax.sharding import PartitionSpec as P

CTX = ("ctx_0", "ctx_1", "ctx_2")
F32 = jnp.float32
BF16 = jnp.bfloat16
L = 128


def params():
    return pltpu.CompilerParams(vmem_limit_bytes=48 * 1024 * 1024)


def nn(a, b):
    return lax.dot_general(a, b, (((1,), (0,)), ((), ())), preferred_element_type=F32)


def nt(a, b):
    return lax.dot_general(a, b, (((1,), (1,)), ((), ())), preferred_element_type=F32)


def tn(a, b):
    return lax.dot_general(a, b, (((0,), (0,)), ((), ())), preferred_element_type=F32)


def halves(x):
    high = x.astype(BF16)
    return high, (x - high.astype(F32)).astype(BF16)


def np_halves(x):
    high = np.asarray(x, np.float32).astype(BF16)
    low = np.asarray(x - high.astype(np.float64), np.float32).astype(BF16)
    return high, low


def tables():
    whole = 2 * L * L
    k = np.arange(L) + 0.5
    n = np.arange(L)
    first = 2.0 * np.pi * np.outer(k, n) / (2 * L)
    one = np.concatenate([np.cos(first), -np.sin(first)], axis=0)
    one_high, one_low = np_halves(one)
    forward = np.concatenate([one_high, one_low], axis=1)
    back_high, back_low = np_halves(one.T * (2.0 / whole))
    twist = 2.0 * np.pi * np.outer(k, n) / whole
    cos_twist = np.cos(twist).astype(np.float32)
    sin_twist = np.sin(twist).astype(np.float32)
    second = 2.0 * np.pi * (np.outer(n, n) % L) / L
    cos_two, sin_two = np.cos(second), np.sin(second)
    two = np.block([[cos_two, -sin_two], [sin_two, cos_two]])
    two_high, two_low = np_halves(two)
    return (forward, back_high, back_low, cos_twist, sin_twist, two_high, two_low)


def pre_kernel(grads, weight, lq, sq, prod, lk, lf, out, grad_two, rows):
    total = nt(grads[0], weight[:, 0:512])
    for part in range(1, 4):
        total += nt(grads[part], weight[:, 512 * part : 512 * (part + 1)])
    grad_low = total.astype(BF16)
    grad_two[...] = grad_low
    gated = grad_low.astype(F32) * lq[...].astype(F32)
    gate = lk[...].astype(F32) * sq[...].astype(F32)
    for place, value in enumerate((lf[...].astype(F32), prod[...].astype(F32), gate, gated)):
        for c in range(4):
            rows[pl.ds(4 * place + c, L, stride=16), :] = value[:, L * c : L * (c + 1)].T
    out[...] = rows[...].reshape(L, 16, L).astype(BF16)


def tap_loop(ext, taps, extended_rows, causal, finish):
    def chunk(index, carry):
        lanes = pl.ds(pl.multiple_of(index * L, L), L)
        total = jnp.zeros((L, L), F32)
        for shift in range(8):
            if causal:
                extended_rows[8:256, :] = ext[8 - shift : 256 - shift, lanes]
            else:
                extended_rows[0:248, :] = ext[shift : 248 + shift, lanes]
            for group in range(16):
                start = L - 8 * group if causal else 8 * group
                tap = 8 * group + shift
                total += taps[tap : tap + 1, lanes] * extended_rows[start : start + L, :]
        finish(lanes, total)
        return carry

    lax.fori_loop(0, 4, chunk, 0)


def mix_kernel(before, prod, taps_in, out, ext, taps, extended_rows):
    ext[0:L, :] = before[...].astype(F32)
    ext[L : 2 * L, :] = prod[...].astype(F32)
    taps[...] = taps_in[...].astype(F32)

    def finish(lanes, total):
        out[:, lanes] = total

    tap_loop(ext, taps, extended_rows, True, finish)


def last_kernel(gated, after, taps_in, sk, sv, key_out, value_out, ext, taps, extended_rows):
    ext[0:L, :] = gated[...].astype(F32)
    ext[L : 2 * L, :] = after[...].astype(F32)
    taps[...] = taps_in[...].astype(F32)

    def finish(lanes, total):
        key_out[:, lanes] = (total * sv[:, lanes].astype(F32)).astype(BF16)
        value_out[:, lanes] = (total * sk[:, lanes].astype(F32)).astype(BF16)

    tap_loop(ext, taps, extended_rows, False, finish)


def spectral_kernel(
    place, arrived, taps_in, forward, back_high, back_low, cos_ref, sin_ref, high_ref, low_ref,
    out, rows,
):
    rows[0:16, :] = jnp.zeros((16, L), F32)
    rows[16:, :] = arrived[...].astype(F32).reshape(16 * L, L)

    def array(a, c, back=0):
        return rows[pl.ds(16 * (1 - back) + 4 * a + c, L, stride=16), :]

    row_index = lax.broadcasted_iota(jnp.int32, (L, L), 0)
    lane_index = lax.broadcasted_iota(jnp.int32, (L, L), 1)
    chosen = (lax.broadcasted_iota(jnp.int32, (16, L), 1) == place[0]).astype(F32).astype(BF16)
    flip = (row_index + lane_index == L - 1).astype(F32).astype(BF16)
    prods, earlier, gates = [], [], []
    product_two = []
    for c in range(4):
        prods.append(array(1, c).astype(BF16))
        earlier.append(array(1, c, 1).astype(BF16))
        gates.append(array(2, c))
        taps = nt(chosen, taps_in[:, L * c : L * (c + 1)])[0:1, :]
        turned = pltpu.roll(jnp.broadcast_to(taps, (L, L)), 0, 1, stride=1, stride_axis=0)
        own = jnp.where(lane_index >= row_index, turned, 0.0).astype(BF16)
        other = jnp.where(lane_index < row_index, turned, 0.0).astype(BF16)
        short_mix = nn(prods[c], own) + nn(earlier[c], other)
        product_two.append((gates[c] * short_mix).astype(BF16))

    cos_t, sin_t = cos_ref[...], sin_ref[...]
    high, low = high_ref[...], low_ref[...]

    def spectrum(columns):
        both = jnp.concatenate(columns, axis=1)
        first = nn(forward[...], jnp.concatenate([both, both], axis=0))
        turned = []
        for c in range(4):
            real = first[0:L, L * c : L * (c + 1)]
            imag = first[L : 2 * L, L * c : L * (c + 1)]
            turned.append(
                jnp.concatenate(
                    [real * cos_t + imag * sin_t, imag * cos_t - real * sin_t], axis=1
                )
            )
        coarse, fine = halves(jnp.concatenate(turned, axis=0))
        result = nn(coarse, high) + nn(coarse, low) + nn(fine, high)
        return result[:, 0:L], result[:, L : 2 * L]

    def restore(real, imag):
        coarse, fine = halves(jnp.concatenate([real, imag], axis=1))
        turned = nt(coarse, high) + nt(coarse, low) + nt(fine, high)
        columns = []
        for c in range(4):
            real = turned[L * c : L * (c + 1), 0:L]
            imag = turned[L * c : L * (c + 1), L : 2 * L]
            columns.append(
                jnp.concatenate(
                    [real * cos_t - imag * sin_t, imag * cos_t + real * sin_t], axis=0
                )
            )
        coarse, fine = halves(jnp.concatenate(columns, axis=1))
        return nn(back_high[...], coarse) + nn(back_high[...], fine) + nn(back_low[...], coarse)

    real_h, imag_h = spectrum([array(0, c).astype(BF16) for c in range(4)])
    real_g, imag_g = spectrum([array(3, c).astype(BF16) for c in range(4)])
    real_u, imag_u = spectrum(product_two)
    back_two = restore(real_h * real_g + imag_h * imag_g, real_h * imag_g - imag_h * real_g)
    long_mix = restore(real_h * real_u - imag_h * imag_u, real_h * imag_u + imag_h * real_u)
    filter_two = restore(real_u * real_g + imag_u * imag_g, real_u * imag_g - imag_u * real_g)
    scaling = 1.0 / L
    for c in range(4):
        part = slice(L * c, L * (c + 1))
        gated_one = (back_two[:, part] * gates[c]).astype(BF16)
        now = tn(nn(prods[c], flip).astype(BF16), gated_one)
        then = tn(nn(earlier[c], flip).astype(BF16), gated_one)
        pairs = jnp.where(lane_index >= L - 1 - row_index, now, then)
        turned = pltpu.roll(pairs, 1, 1, stride=1, stride_axis=0)
        filter_one = jnp.sum(turned, axis=0, keepdims=True) * scaling
        rows[pl.ds(c, L, stride=16), :] = back_two[:, part]
        rows[pl.ds(4 + c, L, stride=16), :] = long_mix[:, part]
        rows[pl.ds(8 + c, L, stride=16), :] = filter_two[:, part] * scaling
        rows[pl.ds(12 + c, L, stride=16), :] = jnp.broadcast_to(filter_one, (L, L))
    out[...] = rows[0 : 16 * L, :].reshape(L, 16, L).astype(BF16)


def post_kernel(
    arrived, grad_two, short_mix, sq, lk, query_out, key_out, filter_out, taps_out, short_out,
    gated_out, rows,
):
    rows[...] = arrived[...].astype(F32).reshape(16 * L, L)

    def array(a, c):
        return rows[pl.ds(4 * a + c, L, stride=16), :].T

    for c in range(4):
        lanes = slice(L * c, L * (c + 1))
        back_two = array(0, c)
        mix = short_mix[:, lanes]
        query = sq[:, lanes].astype(F32)
        mixed = (query * mix).astype(BF16).astype(F32)
        mixed_grad = (back_two * lk[:, lanes].astype(F32)).astype(BF16).astype(F32)
        gated_out[:, lanes] = (mixed_grad * query).astype(BF16)
        short_out[:, lanes] = (mixed_grad * mix).astype(BF16)
        key_out[:, lanes] = (back_two * mixed).astype(BF16)
        query_out[:, lanes] = (grad_two[:, lanes].astype(F32) * array(1, c)).astype(BF16)
        filter_out[:, lanes] = array(2, c).astype(BF16)
        taps_out[:, lanes] = array(3, c).astype(BF16)


def passed_along(block, axis, distance):
    devices = range(lax.axis_size(axis))
    route = [(i - distance, i) for i in devices if i - distance in devices]
    return lax.ppermute(block, axis, route)


def body(sq, sk, sv, taps, lq, lk, lf, weight, out_grad):
    block = jax.ShapeDtypeStruct((L, 4 * L), BF16)
    payload = jax.ShapeDtypeStruct((L, 16, L), BF16)
    peers = lax.axis_size("tp")
    grads = lax.all_to_all(
        jnp.broadcast_to(out_grad[None], (peers, *out_grad.shape)), "tp", 0, 0, tiled=True
    )
    prod = (sk.astype(F32) * sv.astype(F32)).astype(BF16)
    before = passed_along(prod, CTX, 1)
    sent, grad_two = pl.pallas_call(
        pre_kernel,
        out_shape=(payload, block),
        scratch_shapes=[pltpu.VMEM((16 * L, L), F32)],
        compiler_params=params(),
        name="pre",
    )(grads, weight, lq, sq, prod, lk, lf)
    arrived = lax.all_to_all(sent, CTX, 0, 0, tiled=True)
    conv_scratch = [
        pltpu.VMEM((2 * L, 4 * L), F32), pltpu.VMEM((L, 4 * L), F32), pltpu.VMEM((2 * L, L), F32)
    ]
    short_mix = pl.pallas_call(
        mix_kernel,
        out_shape=jax.ShapeDtypeStruct((L, 4 * L), F32),
        scratch_shapes=conv_scratch,
        compiler_params=params(),
        name="mix",
    )(before, prod, taps)
    place = lax.axis_index(CTX).astype(jnp.int32).reshape(1)
    vmem = pl.BlockSpec(memory_space=pltpu.VMEM)
    returned = pl.pallas_call(
        spectral_kernel,
        out_shape=payload,
        in_specs=[pl.BlockSpec(memory_space=pltpu.SMEM)] + [vmem] * 9,
        scratch_shapes=[pltpu.VMEM((16 * L + 16, L), F32)],
        compiler_params=params(),
        name="spectral",
    )(place, arrived, taps, *(jnp.asarray(t) for t in tables()))
    landed = lax.all_to_all(returned, CTX, 0, 0, tiled=True)
    query_out, key_out, filter_out, taps_out, short_out, gated = pl.pallas_call(
        post_kernel,
        out_shape=(block,) * 6,
        scratch_shapes=[pltpu.VMEM((16 * L, L), F32)],
        compiler_params=params(),
        name="post",
    )(landed, grad_two, short_mix, sq, lk)
    after = passed_along(gated, CTX, -1)
    short_key_grad, short_value_grad = pl.pallas_call(
        last_kernel,
        out_shape=(block, block),
        scratch_shapes=conv_scratch,
        compiler_params=params(),
        name="last",
    )(gated, after, taps, sk, sv)
    return (
        short_out, short_key_grad, short_value_grad, taps_out, query_out, key_out, filter_out
    )


def solution(mesh):
    split = Mesh(
        mesh.devices.reshape(16, 4, 2, mesh.shape["tp"]), ("ctx_0", "ctx_1", "ctx_2", "tp")
    )
    rows = P(CTX, "tp")
    columns = P(None, "tp")
    return jax.shard_map(
        body,
        mesh=split,
        in_specs=(rows, rows, rows, columns, rows, rows, rows, P("tp", None), rows),
        out_specs=(rows, rows, rows, columns, rows, rows, rows),
        check_vma=False,
    )
```

profile of v0, /device:TPU:25, one launch (start us, length us, event | category | flops | bytes accessed | tf_op | source)
XLA Modules:
  0.0 130.2 jit_solution(14221190402094985204)
XLA Ops:
  0.6 0.0 copy-start.3
  0.6 0.0 copy-start.2
  0.7 0.0 copy-start.7
  0.7 0.0 copy-start.6
  0.7 1.8 %broadcast_in_dim.2 = bf16[4,128,512]{2,1,0:T(8,128)(2,1)} broadcast(bf16[128,512]{1,0:T(8,128)(2,1)} %param.24), dimensions={1,2} | broadcast | bytes 655360 | tf_op jit(solution)/shard_map/broadcast_in_dim | solution.py:238
  2.5 4.0 %all-to-all-start = ((bf16[4,128,512]{2,1,0:T(8,128)(2,1)}), bf16[4,128,512]{2,1,0:T(8,128)(2,1)S(1)}, u32[]{:S(2)}, u32[]{:S(2)}) async-start(bf16[4,128,512]{2,1,0:T(8,128)(2,1)} %broadcast_in_dim.2), calls=%async_computation | async-start | bytes 1048576 | tf_op jit(solution)/shard_map/all_to_all | solution.py:237
  6.5 1.0 multiply_convert_fusion.prod
  7.5 7.3 %all-to-all-done.grads = bf16[4,128,512]{2,1,0:T(8,128)(2,1)S(1)} async-done(((bf16[4,128,512]{2,1,0:T(8,128)(2,1)}), bf16[4,128,512]{2,1,0:T(8,128)(2,1)S(1)}, u32[]{:S(2)}, u32[]{:S(2)}) %all-to-all-start) | async-done | bytes 524320 | tf_op jit(solution)/shard_map/all_to_all | solution.py:237
  14.8 0.0 copy-done.3
  14.8 0.0 copy-done.2
  14.8 0.0 copy-done.7
  14.8 0.0 copy-done.6
  14.8 0.0 copy-start
  14.9 1.6 %copy-done = bf16[512,2048]{1,0:T(8,128)(2,1)S(1)} copy-done((bf16[512,2048]{1,0:T(8,128)(2,1)S(1)}, bf16[512,2048]{1,0:T(8,128)(2,1)}, u32[]{:S(2)}) %copy-start) | copy-done | bytes 2097176
  16.4 0.0 copy-start.1
  16.4 0.0 copy-start.8
  16.4 0.0 copy-start.9
  16.4 0.0 copy-start.10
  16.4 0.0 copy-start.11
  16.5 0.0 copy-start.12
  16.5 0.0 copy-start.13
  16.5 0.0 copy-start.14
  16.5 1.9 %pre.1 = (bf16[128,16,128]{2,1,0:T(8,128)(2,1)}, bf16[128,512]{1,0:T(8,128)(2,1)S(1)}) custom-call(bf16[4,128,512]{2,1,0:T(8,128)(2,1)S(1)} %all-to-all-done.grads, bf16[512,2048]{1,0:T(8,128)(2,1)S(1)} %copy-done, bf16[128,512]{1,0:T(8,128)(2,1)S(1)} %copy-done.6, bf16[128,512]{1,0:T(8,128)(2,1)S(1)} %copy-done.2, ...), custom_call_target="tpu_custom_call" | custom-call | tf_op jit(solution)/shard_map/pre/pallas_call | solution.py:242
  18.4 21.0 %all-to-all-start.1 = ((bf16[128,16,128]{2,1,0:T(8,128)(2,1)}), bf16[128,16,128]{2,1,0:T(8,128)(2,1)S(1)}, u32[]{:S(2)}, u32[]{:S(2)}) async-start(bf16[128,16,128]{2,1,0:T(8,128)(2,1)} %get-tuple-element.17), calls=%async_computation.1 | async-start | bytes 1048576 | tf_op jit(solution)/shard_map/all_to_all | solution.py:249
  39.4 32.7 %all-to-all-done.1.arrived = bf16[128,16,128]{2,1,0:T(8,128)(2,1)S(1)} async-done(((bf16[128,16,128]{2,1,0:T(8,128)(2,1)}), bf16[128,16,128]{2,1,0:T(8,128)(2,1)S(1)}, u32[]{:S(2)}, u32[]{:S(2)}) %all-to-all-start.1) | async-done | bytes 524320 | tf_op jit(solution)/shard_map/all_to_all | solution.py:249
  72.1 0.0 copy-done.1
  72.1 0.0 copy-done.8
  72.1 0.0 copy-done.9
  72.1 0.0 copy-done.10
  72.1 0.0 copy-done.11
  72.1 0.0 copy-done.12
  72.1 0.0 copy-done.13
  72.1 0.0 copy-done.14
  72.1 0.0 copy-start.4
  72.2 0.0 copy-start.5
  72.2 5.0 %spectral.1 = bf16[128,16,128]{2,1,0:T(8,128)(2,1)} custom-call(s32[1]{0:T(128)} %bitcast.place, bf16[128,16,128]{2,1,0:T(8,128)(2,1)S(1)} %all-to-all-done.1.arrived, bf16[128,512]{1,0:T(8,128)(2,1)S(1)} %copy-done.1, bf16[256,256]{1,0:T(8,128)(2,1)S(1)} %copy-done.10, bf16[128,256]{1,0:T(8,128)(2,1)S(1)} %copy-done.14, bf16[128,256]{1,0:T(8,128)(2,1)S(1)} %copy-done.13, ...), custom_call_target="tpu_custom_call" | custom-call | tf_op jit(solution)/shard_map/spectral/pallas_call | solution.py:262
  77.2 7.2 %all-to-all-start.2 = ((bf16[128,16,128]{2,1,0:T(8,128)(2,1)}), bf16[128,16,128]{2,1,0:T(8,128)(2,1)S(1)}, u32[]{:S(2)}, u32[]{:S(2)}) async-start(bf16[128,16,128]{2,1,0:T(8,128)(2,1)} %spectral.1), calls=%async_computation.2 | async-start | bytes 1048576 | tf_op jit(solution)/shard_map/all_to_all | solution.py:270
  84.4 3.4 %collective-permute-start = (bf16[128,512]{1,0:T(8,128)(2,1)S(1)}, bf16[128,512]{1,0:T(8,128)(2,1)S(1)}, u32[]{:S(2)}, u32[]{:S(2)}) collective-permute-start(bf16[128,512]{1,0:T(8,128)(2,1)S(1)} %multiply_convert_fusion.prod), channel_id=1, source_target_pairs={{0,4},{4,8},{8,12},{12,16},{16,20},{20,24},{24,28},{28,32},{32,36}... | collective-permute-start | bytes 393224 | tf_op jit(solution)/shard_map/ppermute | solution.py:230
  87.8 16.9 %collective-permute-done.before = bf16[128,512]{1,0:T(8,128)(2,1)S(1)} collective-permute-done((bf16[128,512]{1,0:T(8,128)(2,1)S(1)}, bf16[128,512]{1,0:T(8,128)(2,1)S(1)}, u32[]{:S(2)}, u32[]{:S(2)}) %collective-permute-start) | collective-permute-done | bytes 131104 | tf_op jit(solution)/shard_map/ppermute | solution.py:230
  104.7 2.7 %mix.1.short_mix = f32[128,512]{1,0:T(8,128)S(1)} custom-call(bf16[128,512]{1,0:T(8,128)(2,1)S(1)} %collective-permute-done.before, bf16[128,512]{1,0:T(8,128)(2,1)S(1)} %multiply_convert_fusion.prod, bf16[128,512]{1,0:T(8,128)(2,1)S(1)} %copy-done.1), custom_call_target="tpu_custom_call" | custom-call | tf_op jit(solution)/shard_map/mix/pallas_call | solution.py:253
  107.4 9.7 %all-to-all-done.2.arrived = bf16[128,16,128]{2,1,0:T(8,128)(2,1)S(1)} async-done(((bf16[128,16,128]{2,1,0:T(8,128)(2,1)}), bf16[128,16,128]{2,1,0:T(8,128)(2,1)S(1)}, u32[]{:S(2)}, u32[]{:S(2)}) %all-to-all-start.2) | async-done | bytes 524320 | tf_op jit(solution)/shard_map/all_to_all | solution.py:270
  117.1 1.3 post.1
  118.4 2.2 %collective-permute-start.1 = (bf16[128,512]{1,0:T(8,128)(2,1)S(1)}, bf16[128,512]{1,0:T(8,128)(2,1)S(1)}, u32[]{:S(2)}, u32[]{:S(2)}) collective-permute-start(bf16[128,512]{1,0:T(8,128)(2,1)S(1)} %get-tuple-element.20.gated), channel_id=1, source_target_pairs={{4,0},{8,4},{12,8},{16,12},{20,16},{24,20},{28,24},{32,28},{36,32}... | collective-permute-start | bytes 393224 | tf_op jit(solution)/shard_map/ppermute | solution.py:230
  120.6 6.2 %collective-permute-done.1.after = bf16[128,512]{1,0:T(8,128)(2,1)S(1)} collective-permute-done((bf16[128,512]{1,0:T(8,128)(2,1)S(1)}, bf16[128,512]{1,0:T(8,128)(2,1)S(1)}, u32[]{:S(2)}, u32[]{:S(2)}) %collective-permute-start.1) | collective-permute-done | bytes 131104 | tf_op jit(solution)/shard_map/ppermute | solution.py:230
  126.8 0.0 copy-done.4
  126.8 0.0 copy-done.5
  126.8 3.4 %last.1 = (bf16[128,512]{1,0:T(8,128)(2,1)}, bf16[128,512]{1,0:T(8,128)(2,1)}) custom-call(bf16[128,512]{1,0:T(8,128)(2,1)S(1)} %get-tuple-element.20.gated, bf16[128,512]{1,0:T(8,128)(2,1)S(1)} %collective-permute-done.1.after, bf16[128,512]{1,0:T(8,128)(2,1)S(1)} %copy-done.1, bf16[128,512]{1,0:T(8,128)(2,1)S(1)} %copy-done.5, bf16[128,512]{1,0:T(8,128)(2,1)S(1)} %copy-done.4), custom_call_target="tpu_custom_call" | custom-call | tf_op jit(solution)/shard_map/last/pallas_call | solution.py:279
Async XLA Ops:
  0.6 14.2 %copy-start.3 = (bf16[128,512]{1,0:T(8,128)(2,1)S(1)}, bf16[128,512]{1,0:T(8,128)(2,1)}, u32[]{:S(2)}) copy-start(bf16[128,512]{1,0:T(8,128)(2,1)} %lk.3) | copy-start | bytes 393220
  0.6 14.2 %copy-start.2 = (bf16[128,512]{1,0:T(8,128)(2,1)S(1)}, bf16[128,512]{1,0:T(8,128)(2,1)}, u32[]{:S(2)}) copy-start(bf16[128,512]{1,0:T(8,128)(2,1)} %sq.3) | copy-start | bytes 393220
  0.7 14.2 %copy-start.7 = (bf16[128,512]{1,0:T(8,128)(2,1)S(1)}, bf16[128,512]{1,0:T(8,128)(2,1)}, u32[]{:S(2)}) copy-start(bf16[128,512]{1,0:T(8,128)(2,1)} %lf.1) | copy-start | bytes 393220
  0.7 14.2 %copy-start.6 = (bf16[128,512]{1,0:T(8,128)(2,1)S(1)}, bf16[128,512]{1,0:T(8,128)(2,1)}, u32[]{:S(2)}) copy-start(bf16[128,512]{1,0:T(8,128)(2,1)} %lq.1) | copy-start | bytes 393220
  2.5 12.3 %all-to-all-start = ((bf16[4,128,512]{2,1,0:T(8,128)(2,1)}), bf16[4,128,512]{2,1,0:T(8,128)(2,1)S(1)}, u32[]{:S(2)}, u32[]{:S(2)}) async-start(bf16[4,128,512]{2,1,0:T(8,128)(2,1)} %broadcast_in_dim.2), calls=%async_computation | async-start | bytes 1048576 | tf_op jit(solution)/shard_map/all_to_all | solution.py:237
  14.8 1.6 %copy-start = (bf16[512,2048]{1,0:T(8,128)(2,1)S(1)}, bf16[512,2048]{1,0:T(8,128)(2,1)}, u32[]{:S(2)}) copy-start(bf16[512,2048]{1,0:T(8,128)(2,1)} %weight.1) | copy-start | bytes 6291460
  16.4 55.7 %copy-start.1 = (bf16[128,512]{1,0:T(8,128)(2,1)S(1)}, bf16[128,512]{1,0:T(8,128)(2,1)}, u32[]{:S(2)}) copy-start(bf16[128,512]{1,0:T(8,128)(2,1)} %taps_in.5) | copy-start | bytes 393220
  16.4 55.7 %copy-start.8 = (bf16[256,256]{1,0:T(8,128)(2,1)S(1)}, bf16[256,256]{1,0:T(8,128)(2,1)}, u32[]{:S(2)}) copy-start(bf16[256,256]{1,0:T(8,128)(2,1)} %constant.40.clone.low_ref) | copy-start | bytes 393220
  16.4 55.7 %copy-start.9 = (bf16[256,256]{1,0:T(8,128)(2,1)S(1)}, bf16[256,256]{1,0:T(8,128)(2,1)}, u32[]{:S(2)}) copy-start(bf16[256,256]{1,0:T(8,128)(2,1)} %constant.39.clone.high_ref) | copy-start | bytes 393220
  16.4 55.7 %copy-start.10 = (bf16[256,256]{1,0:T(8,128)(2,1)S(1)}, bf16[256,256]{1,0:T(8,128)(2,1)}, u32[]{:S(2)}) copy-start(bf16[256,256]{1,0:T(8,128)(2,1)} %constant.34.clone.forward) | copy-start | bytes 393220
  16.4 55.7 %copy-start.11 = (f32[128,128]{1,0:T(8,128)S(1)}, f32[128,128]{1,0:T(8,128)}, u32[]{:S(2)}) copy-start(f32[128,128]{1,0:T(8,128)} %constant.38.clone.sin_ref) | copy-start | bytes 196612
  16.5 55.7 %copy-start.12 = (f32[128,128]{1,0:T(8,128)S(1)}, f32[128,128]{1,0:T(8,128)}, u32[]{:S(2)}) copy-start(f32[128,128]{1,0:T(8,128)} %constant.37.clone.cos_ref) | copy-start | bytes 196612
  16.5 55.7 %copy-start.13 = (bf16[128,256]{1,0:T(8,128)(2,1)S(1)}, bf16[128,256]{1,0:T(8,128)(2,1)}, u32[]{:S(2)}) copy-start(bf16[128,256]{1,0:T(8,128)(2,1)} %constant.36.clone.back_low) | copy-start | bytes 196612
  16.5 55.7 %copy-start.14 = (bf16[128,256]{1,0:T(8,128)(2,1)S(1)}, bf16[128,256]{1,0:T(8,128)(2,1)}, u32[]{:S(2)}) copy-start(bf16[128,256]{1,0:T(8,128)(2,1)} %constant.35.clone.back_high) | copy-start | bytes 196612
  18.4 53.7 %all-to-all-start.1 = ((bf16[128,16,128]{2,1,0:T(8,128)(2,1)}), bf16[128,16,128]{2,1,0:T(8,128)(2,1)S(1)}, u32[]{:S(2)}, u32[]{:S(2)}) async-start(bf16[128,16,128]{2,1,0:T(8,128)(2,1)} %get-tuple-element.17), calls=%async_computation.1 | async-start | bytes 1048576 | tf_op jit(solution)/shard_map/all_to_all | solution.py:249
  72.1 54.6 %copy-start.4 = (bf16[128,512]{1,0:T(8,128)(2,1)S(1)}, bf16[128,512]{1,0:T(8,128)(2,1)}, u32[]{:S(2)}) copy-start(bf16[128,512]{1,0:T(8,128)(2,1)} %sv.1) | copy-start | bytes 393220
  72.2 54.6 %copy-start.5 = (bf16[128,512]{1,0:T(8,128)(2,1)S(1)}, bf16[128,512]{1,0:T(8,128)(2,1)}, u32[]{:S(2)}) copy-start(bf16[128,512]{1,0:T(8,128)(2,1)} %sk.1) | copy-start | bytes 393220
  77.2 39.9 %all-to-all-start.2 = ((bf16[128,16,128]{2,1,0:T(8,128)(2,1)}), bf16[128,16,128]{2,1,0:T(8,128)(2,1)S(1)}, u32[]{:S(2)}, u32[]{:S(2)}) async-start(bf16[128,16,128]{2,1,0:T(8,128)(2,1)} %spectral.1), calls=%async_computation.2 | async-start | bytes 1048576 | tf_op jit(solution)/shard_map/all_to_all | solution.py:270
  84.4 20.3 %collective-permute-start = (bf16[128,512]{1,0:T(8,128)(2,1)S(1)}, bf16[128,512]{1,0:T(8,128)(2,1)S(1)}, u32[]{:S(2)}, u32[]{:S(2)}) collective-permute-start(bf16[128,512]{1,0:T(8,128)(2,1)S(1)} %multiply_convert_fusion.prod), channel_id=1, source_target_pairs={{0,4},{4,8},{8,12},{12,16},{16,20},{20,24},{24,28},{28,32},{32,36}... | collective-permute-start | bytes 393224 | tf_op jit(solution)/shard_map/ppermute | solution.py:230
  118.4 8.4 %collective-permute-start.1 = (bf16[128,512]{1,0:T(8,128)(2,1)S(1)}, bf16[128,512]{1,0:T(8,128)(2,1)S(1)}, u32[]{:S(2)}, u32[]{:S(2)}) collective-permute-start(bf16[128,512]{1,0:T(8,128)(2,1)S(1)} %get-tuple-element.20.gated), channel_id=1, source_target_pairs={{4,0},{8,4},{12,8},{16,12},{20,16},{24,20},{28,24},{32,28},{36,32}... | collective-permute-start | bytes 393224 | tf_op jit(solution)/shard_map/ppermute | solution.py:230
where the time goes:
time: 131 us; the launch traced here: 130 us
  waiting for transfers between devices  72.9 us (56%)
  starting transfers between devices  37.7 us (29%)
  Pallas kernels  14.3 us (11%)
  local copies, waits for them, and re-layouts  3.46 us (3%)
    all_to_all x1, waiting for transfers between devices, body(): arrived = lax.all_to_all(sent, CTX, 0, 0, tiled=True)  32.7 us
    ppermute x2, waiting for transfers between devices, passed_along(): return lax.ppermute(block, axis, route)  23.1 us
    all_to_all x1, starting transfers between devices, body(): arrived = lax.all_to_all(sent, CTX, 0, 0, tiled=True)  21 us
    all_to_all x1, waiting for transfers between devices, body(): landed = lax.all_to_all(returned, CTX, 0, 0, tiled=True)  9.75 us
    all_to_all x1, waiting for transfers between devices, body(): lax.all_to_all(jnp.broadcast_to(out_grad[None], (peers, *out_grad.shape))...  7.32 us
    all_to_all x1, starting transfers between devices, body(): landed = lax.all_to_all(returned, CTX, 0, 0, tiled=True)  7.18 us
    ppermute x2, starting transfers between devices, passed_along(): return lax.ppermute(block, axis, route)  5.54 us
    pallas_call x1, Pallas kernels, body(): pl.pallas_call(spectral_kernel, out_shape=payload, in_specs=[pl.BlockSpec...  5.02 us
  transfers between devices with their start and end apart: 5, of which 5 were waited for; matrix products, arithmetic and copies ran while one was open for 1% of the time, Pallas kernels for 2%

commit v1 on v0

--- a/solution.py
+++ b/solution.py
@@ -1,5 +1,3 @@
-import math
-
 import jax
 import jax.numpy as jnp
 import numpy as np
@@ -9,6 +7,7 @@
 from jax.sharding import Mesh
 from jax.sharding import PartitionSpec as P
 
+
 CTX = ("ctx_0", "ctx_1", "ctx_2")
 F32 = jnp.float32
 BF16 = jnp.bfloat16
@@ -16,7 +15,7 @@
 
 
 def params():
-    return pltpu.CompilerParams(vmem_limit_bytes=48 * 1024 * 1024)
+    return pltpu.CompilerParams(vmem_limit_bytes=24 * 1024 * 1024)
 
 
 def nn(a, b):
@@ -58,43 +57,102 @@
     cos_two, sin_two = np.cos(second), np.sin(second)
     two = np.block([[cos_two, -sin_two], [sin_two, cos_two]])
     two_high, two_low = np_halves(two)
-    return (forward, back_high, back_low, cos_twist, sin_twist, two_high, two_low)
-
-
-def pre_kernel(grads, weight, lq, sq, prod, lk, lf, out, grad_two, rows):
+    return (forward, two_high, two_low, cos_twist, sin_twist, back_high, back_low)
+
+
+def far(array):
+    return pltpu.with_memory_space_constraint(array, pltpu.HBM)
+
+
+def fetch(sources, targets, marks):
+    copies = [
+        pltpu.make_async_copy(source, target, marks.at[k])
+        for k, (source, target) in enumerate(zip(sources, targets))
+    ]
+    for copy in copies:
+        copy.start()
+    return copies
+
+
+def put(rows, place, value):
+    for c in range(4):
+        rows[pl.ds(4 * place + c, L, stride=16), :] = value[:, L * c : L * (c + 1)].T
+
+
+def spread_kernel(grads, out, grads_v, marks_in, marks_out):
+    parts = [pl.ds(L // 2 * half, L // 2) for half in range(2)]
+    copies = fetch(
+        [grads.at[part, :] for part in parts], [grads_v.at[part, :] for part in parts], marks_in
+    )
+    outward = []
+    for half, part in enumerate(parts):
+        copies[half].wait()
+        outward += fetch(
+            [grads_v.at[part, :]] * 4, [out.at[k, part, :] for k in range(4)], marks_out.at[half]
+        )
+    for copy in outward:
+        copy.wait()
+
+
+def stage_kernel(
+    lf, sk, sv, lk, sq, weight, out, gate, prod, weight_v, rows, out_v, lf_v, sk_v, sv_v, lk_v,
+    sq_v, marks,
+):
+    copies = fetch((lf, sk, sv, lk, sq, weight), (lf_v, sk_v, sv_v, lk_v, sq_v, weight_v), marks)
+    put(rows, 3, jnp.zeros((L, 4 * L), F32))
+    copies[0].wait()
+    put(rows, 0, lf_v[...].astype(F32))
+    copies[1].wait()
+    copies[2].wait()
+    product = (sk_v[...].astype(F32) * sv_v[...].astype(F32)).astype(BF16)
+    prod[...] = product
+    put(rows, 1, product.astype(F32))
+    copies[3].wait()
+    copies[4].wait()
+    put(rows, 2, lk_v[...].astype(F32) * sq_v[...].astype(F32))
+    out_v[...] = rows[...].reshape(L, 16, L).astype(BF16)
+    gate[...] = out_v[:, 8:16, :]
+    copy = pltpu.make_async_copy(out_v, out, marks.at[6])
+    copy.start()
+    copies[5].wait()
+    copy.wait()
+
+
+def join_kernel(grads, gate, weight, lq, staged, out, grad_two, rows, lq_v, out_v, marks):
+    copies = fetch([lq], [lq_v], marks)
+    rows[...] = gate[...].astype(F32).reshape(8 * L, L)
     total = nt(grads[0], weight[:, 0:512])
     for part in range(1, 4):
         total += nt(grads[part], weight[:, 512 * part : 512 * (part + 1)])
     grad_low = total.astype(BF16)
     grad_two[...] = grad_low
-    gated = grad_low.astype(F32) * lq[...].astype(F32)
-    gate = lk[...].astype(F32) * sq[...].astype(F32)
-    for place, value in enumerate((lf[...].astype(F32), prod[...].astype(F32), gate, gated)):
-        for c in range(4):
-            rows[pl.ds(4 * place + c, L, stride=16), :] = value[:, L * c : L * (c + 1)].T
-    out[...] = rows[...].reshape(L, 16, L).astype(BF16)
-
-
-def tap_loop(ext, taps, extended_rows, causal, finish):
+    copies[0].wait()
+    gated = grad_low.astype(F32) * lq_v[...].astype(F32)
+    for c in range(4):
+        rows[pl.ds(4 + c, L, stride=8), :] = gated[:, L * c : L * (c + 1)].T
+    out_v[...] = rows[...].reshape(L, 8, L).astype(BF16)
+    copy = pltpu.make_async_copy(out_v, out.at[:, 8:16, :], marks.at[1])
+    copy.start()
+    copy.wait()
+
+
+def mix_loop(ext, taps, shifted, finish):
     def chunk(index, carry):
         lanes = pl.ds(pl.multiple_of(index * L, L), L)
         total = jnp.zeros((L, L), F32)
         for shift in range(8):
-            if causal:
-                extended_rows[8:256, :] = ext[8 - shift : 256 - shift, lanes]
-            else:
-                extended_rows[0:248, :] = ext[shift : 248 + shift, lanes]
+            shifted[8:256, :] = ext[8 - shift : 256 - shift, lanes]
             for group in range(16):
-                start = L - 8 * group if causal else 8 * group
+                start = L - 8 * group
                 tap = 8 * group + shift
-                total += taps[tap : tap + 1, lanes] * extended_rows[start : start + L, :]
+                total += taps[tap : tap + 1, lanes] * shifted[start : start + L, :]
         finish(lanes, total)
         return carry
 
     lax.fori_loop(0, 4, chunk, 0)
 
 
-def mix_kernel(before, prod, taps_in, out, ext, taps, extended_rows):
+def mix_kernel(before, prod, taps_in, out, ext, taps, shifted):
     ext[0:L, :] = before[...].astype(F32)
     ext[L : 2 * L, :] = prod[...].astype(F32)
     taps[...] = taps_in[...].astype(F32)
@@ -102,23 +160,59 @@
     def finish(lanes, total):
         out[:, lanes] = total
 
-    tap_loop(ext, taps, extended_rows, True, finish)
-
-
-def last_kernel(gated, after, taps_in, sk, sv, key_out, value_out, ext, taps, extended_rows):
-    ext[0:L, :] = gated[...].astype(F32)
-    ext[L : 2 * L, :] = after[...].astype(F32)
+    mix_loop(ext, taps, shifted, finish)
+
+
+def back_loop(ext, taps, shifted, inside, finish):
+    def chunk(index, carry):
+        lanes = pl.ds(pl.multiple_of(index * L, L), L)
+        total = [jnp.zeros((8, L), F32) for _ in range(16)]
+        for shift in range(8):
+            shifted[...] = ext[shift : L + shift, lanes]
+            for group in range(16):
+                tap = taps[8 * group + shift : 8 * group + shift + 1, lanes]
+                for tile in range(16 - group if inside else group + 1):
+                    source = tile + group if inside else tile
+                    place = tile if inside else 15 - group + tile
+                    total[place] += tap * shifted[8 * source : 8 * (source + 1), :]
+        finish(lanes, jnp.concatenate(total, axis=0), index)
+        return carry
+
+    lax.fori_loop(0, 4, chunk, 0)
+
+
+def last_kernel(after, partial, taps_in, sk, sv, key_out, value_out, ext, taps, shifted, key_v, value_v, marks):
+    ext[0:8, :] = jnp.zeros((8, 4 * L), F32)
+    ext[8:, :] = after[...].astype(F32)
     taps[...] = taps_in[...].astype(F32)
 
-    def finish(lanes, total):
-        key_out[:, lanes] = (total * sv[:, lanes].astype(F32)).astype(BF16)
-        value_out[:, lanes] = (total * sk[:, lanes].astype(F32)).astype(BF16)
-
-    tap_loop(ext, taps, extended_rows, False, finish)
+    def outward(lanes, index):
+        return (
+            pltpu.make_async_copy(key_v.at[:, lanes], key_out.at[:, lanes], marks.at[0, index]),
+            pltpu.make_async_copy(value_v.at[:, lanes], value_out.at[:, lanes], marks.at[1, index]),
+        )
+
+    def finish(lanes, total, index):
+        total += partial[:, lanes]
+        key_v[:, lanes] = (total * sv[:, lanes].astype(F32)).astype(BF16)
+        value_v[:, lanes] = (total * sk[:, lanes].astype(F32)).astype(BF16)
+        for copy in outward(lanes, index):
+            copy.start()
+
+    back_loop(ext, taps, shifted, False, finish)
+    for index in range(4):
+        for copy in outward(pl.ds(L * index, L), index):
+            copy.wait()
+
+
+def load_kernel(*refs):
+    count = len(refs) // 2
+    for copy in fetch(refs[:count], refs[count : 2 * count], refs[-1]):
+        copy.wait()
 
 
 def spectral_kernel(
-    place, arrived, taps_in, forward, back_high, back_low, cos_ref, sin_ref, high_ref, low_ref,
+    place, arrived, taps_in, forward, high_ref, low_ref, cos_ref, sin_ref, back_high, back_low,
     out, rows,
 ):
     rows[0:16, :] = jnp.zeros((16, L), F32)
@@ -200,9 +294,20 @@
     out[...] = rows[0 : 16 * L, :].reshape(L, 16, L).astype(BF16)
 
 
+def turn_kernel(arrived, sq, lk, back_out, gated_out, rows):
+    rows[...] = arrived[...].astype(F32).reshape(16 * L, L)
+    for c in range(4):
+        lanes = slice(L * c, L * (c + 1))
+        back_two = rows[pl.ds(c, L, stride=16), :].T
+        back_out[:, lanes] = back_two.astype(BF16)
+        mixed_grad = (back_two * lk[:, lanes].astype(F32)).astype(BF16).astype(F32)
+        gated_out[:, lanes] = (mixed_grad * sq[:, lanes].astype(F32)).astype(BF16)
+
+
 def post_kernel(
-    arrived, grad_two, short_mix, sq, lk, query_out, key_out, filter_out, taps_out, short_out,
-    gated_out, rows,
+    arrived, back, gated, grad_two, short_mix, sq, lk, taps_in, query_out, key_out, filter_out,
+    taps_out, short_out, partial, rows, ext, taps, shifted, query_v, key_v, filter_v, taps_v,
+    short_v, marks,
 ):
     rows[...] = arrived[...].astype(F32).reshape(16 * L, L)
 
@@ -211,17 +316,30 @@
 
     for c in range(4):
         lanes = slice(L * c, L * (c + 1))
-        back_two = array(0, c)
+        back_two = back[:, lanes].astype(F32)
         mix = short_mix[:, lanes]
-        query = sq[:, lanes].astype(F32)
-        mixed = (query * mix).astype(BF16).astype(F32)
+        mixed = (sq[:, lanes].astype(F32) * mix).astype(BF16).astype(F32)
         mixed_grad = (back_two * lk[:, lanes].astype(F32)).astype(BF16).astype(F32)
-        gated_out[:, lanes] = (mixed_grad * query).astype(BF16)
-        short_out[:, lanes] = (mixed_grad * mix).astype(BF16)
-        key_out[:, lanes] = (back_two * mixed).astype(BF16)
-        query_out[:, lanes] = (grad_two[:, lanes].astype(F32) * array(1, c)).astype(BF16)
-        filter_out[:, lanes] = array(2, c).astype(BF16)
-        taps_out[:, lanes] = array(3, c).astype(BF16)
+        short_v[:, lanes] = (mixed_grad * mix).astype(BF16)
+        key_v[:, lanes] = (back_two * mixed).astype(BF16)
+        query_v[:, lanes] = (grad_two[:, lanes].astype(F32) * array(1, c)).astype(BF16)
+        filter_v[:, lanes] = array(2, c).astype(BF16)
+        taps_v[:, lanes] = array(3, c).astype(BF16)
+    copies = fetch(
+        (query_v, key_v, filter_v, taps_v, short_v),
+        (query_out, key_out, filter_out, taps_out, short_out),
+        marks,
+    )
+    ext[0:L, :] = gated[...].astype(F32)
+    ext[L:, :] = jnp.zeros((8, 4 * L), F32)
+    taps[...] = taps_in[...].astype(F32)
+
+    def finish(lanes, total, index):
+        partial[:, lanes] = total
+
+    back_loop(ext, taps, shifted, True, finish)
+    for copy in copies:
+        copy.wait()
 
 
 def passed_along(block, axis, distance):
@@ -233,20 +351,58 @@
 def body(sq, sk, sv, taps, lq, lk, lf, weight, out_grad):
     block = jax.ShapeDtypeStruct((L, 4 * L), BF16)
     payload = jax.ShapeDtypeStruct((L, 16, L), BF16)
-    peers = lax.axis_size("tp")
-    grads = lax.all_to_all(
-        jnp.broadcast_to(out_grad[None], (peers, *out_grad.shape)), "tp", 0, 0, tiled=True
-    )
-    prod = (sk.astype(F32) * sv.astype(F32)).astype(BF16)
+    vmem = pl.BlockSpec(memory_space=pltpu.VMEM)
+    smem = pl.BlockSpec(memory_space=pltpu.SMEM)
+    hbm = pl.BlockSpec(memory_space=pltpu.HBM)
+    tile = pltpu.VMEM((L, 4 * L), BF16)
+    spread = pl.pallas_call(
+        spread_kernel,
+        out_shape=pltpu.HBM((4, L, 4 * L), BF16),
+        in_specs=[hbm],
+        out_specs=hbm,
+        scratch_shapes=[tile, pltpu.SemaphoreType.DMA((2,)), pltpu.SemaphoreType.DMA((2, 4))],
+        compiler_params=params(),
+        name="spread",
+    )(far(out_grad))
+    grads = lax.all_to_all(spread, "tp", 0, 0, tiled=True)
+    sent_shape = pltpu.HBM((L, 16, L), BF16)
+    half = jax.ShapeDtypeStruct((L, 8, L), BF16)
+    staged, gate, prod, weight_v = pl.pallas_call(
+        stage_kernel,
+        out_shape=(sent_shape, half, block, jax.ShapeDtypeStruct((4 * L, 16 * L), BF16)),
+        in_specs=[hbm] * 6,
+        out_specs=(hbm, vmem, vmem, vmem),
+        scratch_shapes=[pltpu.VMEM((16 * L, L), F32), pltpu.VMEM((L, 16, L), BF16)]
+        + [tile] * 5
+        + [pltpu.SemaphoreType.DMA((7,))],
+        compiler_params=params(),
+        name="stage",
+    )(*map(far, (lf, sk, sv, lk, sq, weight)))
     before = passed_along(prod, CTX, 1)
     sent, grad_two = pl.pallas_call(
-        pre_kernel,
-        out_shape=(payload, block),
-        scratch_shapes=[pltpu.VMEM((16 * L, L), F32)],
-        compiler_params=params(),
-        name="pre",
-    )(grads, weight, lq, sq, prod, lk, lf)
+        join_kernel,
+        out_shape=(sent_shape, block),
+        in_specs=[vmem, vmem, vmem, hbm, hbm],
+        out_specs=(hbm, vmem),
+        input_output_aliases={4: 0},
+        scratch_shapes=[
+            pltpu.VMEM((8 * L, L), F32), tile, pltpu.VMEM((L, 8, L), BF16),
+            pltpu.SemaphoreType.DMA((2,)),
+        ],
+        compiler_params=params(),
+        name="join",
+    )(grads, gate, weight_v, far(lq), staged)
     arrived = lax.all_to_all(sent, CTX, 0, 0, tiled=True)
+    constants = [jnp.asarray(t) for t in tables()]
+    loaded = pl.pallas_call(
+        load_kernel,
+        out_shape=tuple(jax.ShapeDtypeStruct(t.shape, t.dtype) for t in constants),
+        in_specs=[hbm] * 7,
+        out_specs=(vmem,) * 7,
+        scratch_shapes=[pltpu.SemaphoreType.DMA((7,))],
+        compiler_params=params(),
+        name="load",
+    )(*map(far, constants))
     conv_scratch = [
         pltpu.VMEM((2 * L, 4 * L), F32), pltpu.VMEM((L, 4 * L), F32), pltpu.VMEM((2 * L, L), F32)
     ]
@@ -258,31 +414,44 @@
         name="mix",
     )(before, prod, taps)
     place = lax.axis_index(CTX).astype(jnp.int32).reshape(1)
-    vmem = pl.BlockSpec(memory_space=pltpu.VMEM)
     returned = pl.pallas_call(
         spectral_kernel,
         out_shape=payload,
-        in_specs=[pl.BlockSpec(memory_space=pltpu.SMEM)] + [vmem] * 9,
+        in_specs=[smem] + [vmem] * 9,
         scratch_shapes=[pltpu.VMEM((16 * L + 16, L), F32)],
         compiler_params=params(),
         name="spectral",
-    )(place, arrived, taps, *(jnp.asarray(t) for t in tables()))
+    )(place, arrived, taps, *loaded)
     landed = lax.all_to_all(returned, CTX, 0, 0, tiled=True)
-    query_out, key_out, filter_out, taps_out, short_out, gated = pl.pallas_call(
+    landed_rows = pltpu.VMEM((16 * L, L), F32)
+    back, gated = pl.pallas_call(
+        turn_kernel,
+        out_shape=(block, block),
+        scratch_shapes=[landed_rows],
+        compiler_params=params(),
+        name="turn",
+    )(landed, sq, lk)
+    after = passed_along(gated, CTX, -1)
+    back_scratch = [
+        pltpu.VMEM((L + 8, 4 * L), F32), pltpu.VMEM((L, 4 * L), F32), pltpu.VMEM((L, L), F32)
+    ]
+    out_block = pltpu.HBM((L, 4 * L), BF16)
+    query_out, key_out, filter_out, taps_out, short_out, partial = pl.pallas_call(
         post_kernel,
-        out_shape=(block,) * 6,
-        scratch_shapes=[pltpu.VMEM((16 * L, L), F32)],
+        out_shape=(out_block,) * 5 + (jax.ShapeDtypeStruct((L, 4 * L), F32),),
+        out_specs=(hbm,) * 5 + (vmem,),
+        scratch_shapes=[landed_rows] + back_scratch + [tile] * 5 + [pltpu.SemaphoreType.DMA((5,))],
         compiler_params=params(),
         name="post",
-    )(landed, grad_two, short_mix, sq, lk)
-    after = passed_along(gated, CTX, -1)
+    )(landed, back, gated, grad_two, short_mix, sq, lk, taps)
     short_key_grad, short_value_grad = pl.pallas_call(
         last_kernel,
-        out_shape=(block, block),
-        scratch_shapes=conv_scratch,
+        out_shape=(out_block,) * 2,
+        out_specs=(hbm,) * 2,
+        scratch_shapes=back_scratch + [tile] * 2 + [pltpu.SemaphoreType.DMA((2, 4))],
         compiler_params=params(),
         name="last",
-    )(gated, after, taps, sk, sv)
+    )(after, partial, taps, sk, sv)
     return (
         short_out, short_key_grad, short_value_grad, taps_out, query_out, key_out, filter_out
     )

time: 131 us -> 127 us (0.969)
  Pallas kernels: 14.3 us -> 19 us
  waiting for transfers between devices: 72.9 us -> 68.4 us
  local copies, waits for them, and re-layouts: 3.46 us -> 0.02 us
    ppermute x2, waiting for transfers between devices: 23.1 us -> 1.65 us  [passed_along(): return lax.ppermute(block, axis, route)]
    all_to_all x1, waiting for transfers between devices: 9.75 us -> 29.4 us  [body(): landed = lax.all_to_all(returned, CTX, 0, 0, tiled=True)]
    pallas_call x4 -> x8, Pallas kernels: 11.6 us -> 16.3 us  [the longest x1 5.02 us: body(): pl.pallas_call(spectral_kernel, out_shape=payload, in_specs=[smem] + [vme...]
    broadcast_in_dim x1 -> x0, local copies, waits for them, and re-layouts: 1.8 us -> none  [body(): jnp.broadcast_to(out_grad[None], (peers, *out_grad.shape))]
    unnamed x30 -> x10, local copies, waits for them, and re-layouts: 1.66 us -> 0.02 us
    all_to_all x1, waiting for transfers between devices: 7.32 us -> 5.91 us  [body(): grads = lax.all_to_all(spread, 'tp', 0, 0, tiled=True)]
  transfers between devices with their start and end apart: 5 -> 5, of which waited for: 5 -> 4; matrix products, arithmetic and copies ran while one was open for 1% -> 0% of each run, Pallas kernels for 2% -> 7%
where the time goes in v1:
time: 127 us; the launch traced here: 126 us
  waiting for transfers between devices  68.4 us (54%)
  starting transfers between devices  38 us (30%)
  Pallas kernels  19 us (15%)
    all_to_all x1, waiting for transfers between devices, body(): arrived = lax.all_to_all(sent, CTX, 0, 0, tiled=True)  31.5 us
    all_to_all x1, waiting for transfers between devices, body(): landed = lax.all_to_all(returned, CTX, 0, 0, tiled=True)  29.4 us
    all_to_all x1, starting transfers between devices, body(): arrived = lax.all_to_all(sent, CTX, 0, 0, tiled=True)  21.1 us
    all_to_all x1, starting transfers between devices, body(): landed = lax.all_to_all(returned, CTX, 0, 0, tiled=True)  7.31 us
    all_to_all x1, waiting for transfers between devices, body(): grads = lax.all_to_all(spread, 'tp', 0, 0, tiled=True)  5.91 us
    ppermute x2, starting transfers between devices, passed_along(): return lax.ppermute(block, axis, route)  5.55 us
    pallas_call x1, Pallas kernels, body(): pl.pallas_call(spectral_kernel, out_shape=payload, in_specs=[smem] + [vme...  5.02 us
    all_to_all x1, starting transfers between devices, body(): grads = lax.all_to_all(spread, 'tp', 0, 0, tiled=True)  4.02 us
  transfers between devices with their start and end apart: 5, of which 4 were waited for; matrix products, arithmetic and copies ran while one was open for 0% of the time, Pallas kernels for 7%

profile of v1, /device:TPU:25, one launch (start us, length us, event | category | flops | bytes accessed | tf_op | source)
XLA Modules:
  0.0 126.2 jit_solution(2764044507999808997)
XLA Ops:
  0.6 1.7 %spread.1 = bf16[4,128,512]{2,1,0:T(8,128)(2,1)} custom-call(bf16[128,512]{1,0:T(8,128)(2,1)} %grads.1), custom_call_target="tpu_custom_call" | custom-call | tf_op jit(solution)/shard_map/spread/pallas_call | solution.py:358
  2.4 4.0 %all-to-all-start = ((bf16[4,128,512]{2,1,0:T(8,128)(2,1)}), bf16[4,128,512]{2,1,0:T(8,128)(2,1)S(1)}, u32[]{:S(2)}, u32[]{:S(2)}) async-start(bf16[4,128,512]{2,1,0:T(8,128)(2,1)} %spread.1), calls=%async_computation | async-start | bytes 1048576 | tf_op jit(solution)/shard_map/all_to_all | solution.py:367
  6.4 2.4 %stage.1 = (bf16[128,16,128]{2,1,0:T(8,128)(2,1)}, bf16[128,8,128]{2,1,0:T(8,128)(2,1)S(1)}, bf16[128,512]{1,0:T(8,128)(2,1)S(1)}, bf16[512,2048]{1,0:T(8,128)(2,1)S(1)}) custom-call(bf16[128,512]{1,0:T(8,128)(2,1)} %lf.1, bf16[128,512]{1,0:T(8,128)(2,1)} %sk.3, bf16[128,512]{1,0:T(8,128)(2,1)} %sv.3, bf16[128,512]{1,0:T(8,128)(2,1)} %lk.5, ...), custom_call_target="tpu_custom_call" | custom-call | tf_op jit(solution)/shard_map/stage/pallas_call | solution.py:370
  8.8 5.9 %all-to-all-done.grads = bf16[4,128,512]{2,1,0:T(8,128)(2,1)S(1)} async-done(((bf16[4,128,512]{2,1,0:T(8,128)(2,1)}), bf16[4,128,512]{2,1,0:T(8,128)(2,1)S(1)}, u32[]{:S(2)}, u32[]{:S(2)}) %all-to-all-start) | async-done | bytes 524320 | tf_op jit(solution)/shard_map/all_to_all | solution.py:367
  14.7 0.0 copy-start
  14.7 1.8 %join.1 = (bf16[128,16,128]{2,1,0:T(8,128)(2,1)}, bf16[128,512]{1,0:T(8,128)(2,1)S(1)}) custom-call(bf16[4,128,512]{2,1,0:T(8,128)(2,1)S(1)} %all-to-all-done.grads, bf16[128,8,128]{2,1,0:T(8,128)(2,1)S(1)} %get-tuple-element.30.gate, bf16[512,2048]{1,0:T(8,128)(2,1)S(1)} %get-tuple-element.31.weight, ...), custom_call_target="tpu_custom_call", output_to_operand_aliasing={{0}: (4, {})} | custom-call | tf_op jit(solution)/shard_map/join/pallas_call | solution.py:382
  16.6 0.0 copy-start.1
  16.6 0.0 copy-start.2
  16.6 21.1 %all-to-all-start.1 = ((bf16[128,16,128]{2,1,0:T(8,128)(2,1)}), bf16[128,16,128]{2,1,0:T(8,128)(2,1)S(1)}, u32[]{:S(2)}, u32[]{:S(2)}) async-start(bf16[128,16,128]{2,1,0:T(8,128)(2,1)} %get-tuple-element.33), calls=%async_computation.1 | async-start | bytes 1048576 | tf_op jit(solution)/shard_map/all_to_all | solution.py:395
  37.8 1.2 load.1
  38.9 31.5 %all-to-all-done.1.arrived = bf16[128,16,128]{2,1,0:T(8,128)(2,1)S(1)} async-done(((bf16[128,16,128]{2,1,0:T(8,128)(2,1)}), bf16[128,16,128]{2,1,0:T(8,128)(2,1)S(1)}, u32[]{:S(2)}, u32[]{:S(2)}) %all-to-all-start.1) | async-done | bytes 524320 | tf_op jit(solution)/shard_map/all_to_all | solution.py:395
  70.5 0.0 copy-done
  70.5 5.0 %spectral.1 = bf16[128,16,128]{2,1,0:T(8,128)(2,1)} custom-call(s32[1]{0:T(128)} %bitcast.place, bf16[128,16,128]{2,1,0:T(8,128)(2,1)S(1)} %all-to-all-done.1.arrived, bf16[128,512]{1,0:T(8,128)(2,1)S(1)} %copy-done, bf16[256,256]{1,0:T(8,128)(2,1)S(1)} %get-tuple-element.34.forward, bf16[256,256]{1,0:T(8,128)(2,1)S(1)} %get-tuple-element.35.high_ref, ...), custom_call_target="tpu_custom_call" | custom-call | tf_op jit(solution)/shard_map/spectral/pallas_call | solution.py:417
  75.5 0.0 copy-start.3
  75.5 0.0 copy-start.4
  75.5 7.3 %all-to-all-start.2 = ((bf16[128,16,128]{2,1,0:T(8,128)(2,1)}), bf16[128,16,128]{2,1,0:T(8,128)(2,1)S(1)}, u32[]{:S(2)}, u32[]{:S(2)}) async-start(bf16[128,16,128]{2,1,0:T(8,128)(2,1)} %spectral.1), calls=%async_computation.2 | async-start | bytes 1048576 | tf_op jit(solution)/shard_map/all_to_all | solution.py:425
  82.8 3.4 %collective-permute-start = (bf16[128,512]{1,0:T(8,128)(2,1)S(1)}, bf16[128,512]{1,0:T(8,128)(2,1)S(1)}, u32[]{:S(2)}, u32[]{:S(2)}) collective-permute-start(bf16[128,512]{1,0:T(8,128)(2,1)S(1)} %get-tuple-element.44.prod), channel_id=1, source_target_pairs={{0,4},{4,8},{8,12},{12,16},{16,20},{20,24},{24,28},{28,32},{32,36}... | collective-permute-start | bytes 393224 | tf_op jit(solution)/shard_map/ppermute | solution.py:348
  86.2 29.4 %all-to-all-done.2.arrived = bf16[128,16,128]{2,1,0:T(8,128)(2,1)S(1)} async-done(((bf16[128,16,128]{2,1,0:T(8,128)(2,1)}), bf16[128,16,128]{2,1,0:T(8,128)(2,1)S(1)}, u32[]{:S(2)}, u32[]{:S(2)}) %all-to-all-start.2) | async-done | bytes 524320 | tf_op jit(solution)/shard_map/all_to_all | solution.py:425
  115.6 0.0 copy-done.1
  115.6 0.0 copy-done.2
  115.6 0.2 turn.1
  115.8 2.2 %collective-permute-start.1 = (bf16[128,512]{1,0:T(8,128)(2,1)S(1)}, bf16[128,512]{1,0:T(8,128)(2,1)S(1)}, u32[]{:S(2)}, u32[]{:S(2)}) collective-permute-start(bf16[128,512]{1,0:T(8,128)(2,1)S(1)} %get-tuple-element.42.gated), channel_id=1, source_target_pairs={{4,0},{8,4},{12,8},{16,12},{20,16},{24,20},{28,24},{32,28},{36,32}... | collective-permute-start | bytes 393224 | tf_op jit(solution)/shard_map/ppermute | solution.py:348
  117.9 0.0 collective-permute-done.before
  118.0 2.7 %mix.1.short_mix = f32[128,512]{1,0:T(8,128)S(1)} custom-call(bf16[128,512]{1,0:T(8,128)(2,1)S(1)} %collective-permute-done.before, bf16[128,512]{1,0:T(8,128)(2,1)S(1)} %get-tuple-element.44.prod, bf16[128,512]{1,0:T(8,128)(2,1)S(1)} %copy-done), custom_call_target="tpu_custom_call" | custom-call | tf_op jit(solution)/shard_map/mix/pallas_call | solution.py:409
  120.6 1.9 %post.1 = (bf16[128,512]{1,0:T(8,128)(2,1)}, bf16[128,512]{1,0:T(8,128)(2,1)}, bf16[128,512]{1,0:T(8,128)(2,1)}, bf16[128,512]{1,0:T(8,128)(2,1)}, bf16[128,512]{1,0:T(8,128)(2,1)}, /*index=5*/f32[128,512]{1,0:T(8,128)S(1)}) custom-call(bf16[128,16,128]{2,1,0:T(8,128)(2,1)S(1)} %all-to-all-done.2.arrived, bf16[128,512]{1,0:T(8,128)(2,1)S(1)} %get-tuple-element.41.back, ...), custom_call_target="tpu_custom_call" | custom-call | tf_op jit(solution)/shard_map/post/pallas_call | solution.py:439
  122.5 1.6 %collective-permute-done.1.after = bf16[128,512]{1,0:T(8,128)(2,1)S(1)} collective-permute-done((bf16[128,512]{1,0:T(8,128)(2,1)S(1)}, bf16[128,512]{1,0:T(8,128)(2,1)S(1)}, u32[]{:S(2)}, u32[]{:S(2)}) %collective-permute-start.1) | collective-permute-done | bytes 131104 | tf_op jit(solution)/shard_map/ppermute | solution.py:348
  124.2 0.0 copy-done.3
  124.2 0.0 copy-done.4
  124.2 2.1 %last.1 = (bf16[128,512]{1,0:T(8,128)(2,1)}, bf16[128,512]{1,0:T(8,128)(2,1)}) custom-call(bf16[128,512]{1,0:T(8,128)(2,1)S(1)} %collective-permute-done.1.after, f32[128,512]{1,0:T(8,128)S(1)} %get-tuple-element.46.partial, bf16[128,512]{1,0:T(8,128)(2,1)S(1)} %copy-done, bf16[128,512]{1,0:T(8,128)(2,1)S(1)} %copy-done.3, bf16[128,512]{1,0:T(8,128)(2,1)S(1)} %copy-done.4), custom_call_target="tpu_custom_call" | custom-call | tf_op jit(solution)/shard_map/last/pallas_call | solution.py:447
Async XLA Ops:
  2.4 12.4 %all-to-all-start = ((bf16[4,128,512]{2,1,0:T(8,128)(2,1)}), bf16[4,128,512]{2,1,0:T(8,128)(2,1)S(1)}, u32[]{:S(2)}, u32[]{:S(2)}) async-start(bf16[4,128,512]{2,1,0:T(8,128)(2,1)} %spread.1), calls=%async_computation | async-start | bytes 1048576 | tf_op jit(solution)/shard_map/all_to_all | solution.py:367
  14.7 55.8 %copy-start = (bf16[128,512]{1,0:T(8,128)(2,1)S(1)}, bf16[128,512]{1,0:T(8,128)(2,1)}, u32[]{:S(2)}) copy-start(bf16[128,512]{1,0:T(8,128)(2,1)} %taps_in.7) | copy-start | bytes 393220
  16.6 99.0 %copy-start.1 = (bf16[128,512]{1,0:T(8,128)(2,1)S(1)}, bf16[128,512]{1,0:T(8,128)(2,1)}, u32[]{:S(2)}) copy-start(bf16[128,512]{1,0:T(8,128)(2,1)} %lk.5) | copy-start | bytes 393220
  16.6 99.0 %copy-start.2 = (bf16[128,512]{1,0:T(8,128)(2,1)S(1)}, bf16[128,512]{1,0:T(8,128)(2,1)}, u32[]{:S(2)}) copy-start(bf16[128,512]{1,0:T(8,128)(2,1)} %sq.5) | copy-start | bytes 393220
  16.6 53.9 %all-to-all-start.1 = ((bf16[128,16,128]{2,1,0:T(8,128)(2,1)}), bf16[128,16,128]{2,1,0:T(8,128)(2,1)S(1)}, u32[]{:S(2)}, u32[]{:S(2)}) async-start(bf16[128,16,128]{2,1,0:T(8,128)(2,1)} %get-tuple-element.33), calls=%async_computation.1 | async-start | bytes 1048576 | tf_op jit(solution)/shard_map/all_to_all | solution.py:395
  75.5 48.7 %copy-start.3 = (bf16[128,512]{1,0:T(8,128)(2,1)S(1)}, bf16[128,512]{1,0:T(8,128)(2,1)}, u32[]{:S(2)}) copy-start(bf16[128,512]{1,0:T(8,128)(2,1)} %sk.3) | copy-start | bytes 393220
  75.5 48.7 %copy-start.4 = (bf16[128,512]{1,0:T(8,128)(2,1)S(1)}, bf16[128,512]{1,0:T(8,128)(2,1)}, u32[]{:S(2)}) copy-start(bf16[128,512]{1,0:T(8,128)(2,1)} %sv.3) | copy-start | bytes 393220
  75.5 40.1 %all-to-all-start.2 = ((bf16[128,16,128]{2,1,0:T(8,128)(2,1)}), bf16[128,16,128]{2,1,0:T(8,128)(2,1)S(1)}, u32[]{:S(2)}, u32[]{:S(2)}) async-start(bf16[128,16,128]{2,1,0:T(8,128)(2,1)} %spectral.1), calls=%async_computation.2 | async-start | bytes 1048576 | tf_op jit(solution)/shard_map/all_to_all | solution.py:425
  82.8 35.1 %collective-permute-start = (bf16[128,512]{1,0:T(8,128)(2,1)S(1)}, bf16[128,512]{1,0:T(8,128)(2,1)S(1)}, u32[]{:S(2)}, u32[]{:S(2)}) collective-permute-start(bf16[128,512]{1,0:T(8,128)(2,1)S(1)} %get-tuple-element.44.prod), channel_id=1, source_target_pairs={{0,4},{4,8},{8,12},{12,16},{16,20},{20,24},{24,28},{28,32},{32,36}... | collective-permute-start | bytes 393224 | tf_op jit(solution)/shard_map/ppermute | solution.py:348
  115.8 8.4 %collective-permute-start.1 = (bf16[128,512]{1,0:T(8,128)(2,1)S(1)}, bf16[128,512]{1,0:T(8,128)(2,1)S(1)}, u32[]{:S(2)}, u32[]{:S(2)}) collective-permute-start(bf16[128,512]{1,0:T(8,128)(2,1)S(1)} %get-tuple-element.42.gated), channel_id=1, source_target_pairs={{4,0},{8,4},{12,8},{16,12},{20,16},{24,20},{28,24},{32,28},{36,32}... | collective-permute-start | bytes 393224 | tf_op jit(solution)/shard_map/ppermute | solution.py:348

commit v2 on v1

--- a/solution.py
+++ b/solution.py
@@ -95,10 +95,12 @@
 
 
 def stage_kernel(
-    lf, sk, sv, lk, sq, weight, out, gate, prod, weight_v, rows, out_v, lf_v, sk_v, sv_v, lk_v,
-    sq_v, marks,
+    lf, sk, sv, lk, sq, lq, weight, out, gate, prod, turned_lq, weight_v, rows, out_v, lf_v, sk_v,
+    sv_v, lk_v, sq_v, lq_v, marks,
 ):
-    copies = fetch((lf, sk, sv, lk, sq, weight), (lf_v, sk_v, sv_v, lk_v, sq_v, weight_v), marks)
+    copies = fetch(
+        (lf, sk, sv, lk, sq, lq, weight), (lf_v, sk_v, sv_v, lk_v, sq_v, lq_v, weight_v), marks
+    )
     put(rows, 3, jnp.zeros((L, 4 * L), F32))
     copies[0].wait()
     put(rows, 0, lf_v[...].astype(F32))
@@ -112,26 +114,26 @@
     put(rows, 2, lk_v[...].astype(F32) * sq_v[...].astype(F32))
     out_v[...] = rows[...].reshape(L, 16, L).astype(BF16)
     gate[...] = out_v[:, 8:16, :]
-    copy = pltpu.make_async_copy(out_v, out, marks.at[6])
+    copy = pltpu.make_async_copy(out_v, out, marks.at[7])
     copy.start()
     copies[5].wait()
+    turned_lq[...] = lq_v[...].astype(F32).T.astype(BF16)
+    copies[6].wait()
     copy.wait()
 
 
-def join_kernel(grads, gate, weight, lq, staged, out, grad_two, rows, lq_v, out_v, marks):
-    copies = fetch([lq], [lq_v], marks)
+def join_kernel(grads, gate, weight, turned_lq, staged, out, grad_two, rows, out_v, mark):
     rows[...] = gate[...].astype(F32).reshape(8 * L, L)
-    total = nt(grads[0], weight[:, 0:512])
+    total = nt(weight[:, 0:512], grads[0])
     for part in range(1, 4):
-        total += nt(grads[part], weight[:, 512 * part : 512 * (part + 1)])
+        total += nt(weight[:, 512 * part : 512 * (part + 1)], grads[part])
     grad_low = total.astype(BF16)
     grad_two[...] = grad_low
-    copies[0].wait()
-    gated = grad_low.astype(F32) * lq_v[...].astype(F32)
-    for c in range(4):
-        rows[pl.ds(4 + c, L, stride=8), :] = gated[:, L * c : L * (c + 1)].T
+    gated = grad_low.astype(F32) * turned_lq[...].astype(F32)
+    for c in range(4):
+        rows[pl.ds(4 + c, L, stride=8), :] = gated[L * c : L * (c + 1), :]
     out_v[...] = rows[...].reshape(L, 8, L).astype(BF16)
-    copy = pltpu.make_async_copy(out_v, out.at[:, 8:16, :], marks.at[1])
+    copy = pltpu.make_async_copy(out_v, out.at[:, 8:16, :], mark)
     copy.start()
     copy.wait()
 
@@ -213,7 +215,7 @@
 
 def spectral_kernel(
     place, arrived, taps_in, forward, high_ref, low_ref, cos_ref, sin_ref, back_high, back_low,
-    out, rows,
+    out, rows, half, out_v, marks,
 ):
     rows[0:16, :] = jnp.zeros((16, L), F32)
     rows[16:, :] = arrived[...].astype(F32).reshape(16 * L, L)
@@ -275,10 +277,22 @@
     real_h, imag_h = spectrum([array(0, c).astype(BF16) for c in range(4)])
     real_g, imag_g = spectrum([array(3, c).astype(BF16) for c in range(4)])
     real_u, imag_u = spectrum(product_two)
+
+    def send(half, group, first, second):
+        for c in range(4):
+            part = slice(L * c, L * (c + 1))
+            half[pl.ds(c, L, stride=8), :] = first[:, part]
+            half[pl.ds(4 + c, L, stride=8), :] = second[:, part]
+        out_v[group] = half[...].reshape(L, 8, L).astype(BF16)
+        copy = pltpu.make_async_copy(
+            out_v.at[group], out.at[:, 8 * group : 8 * (group + 1), :], marks.at[group]
+        )
+        copy.start()
+        return copy
+
+    scaling = 1.0 / L
     back_two = restore(real_h * real_g + imag_h * imag_g, real_h * imag_g - imag_h * real_g)
-    long_mix = restore(real_h * real_u - imag_h * imag_u, real_h * imag_u + imag_h * real_u)
-    filter_two = restore(real_u * real_g + imag_u * imag_g, real_u * imag_g - imag_u * real_g)
-    scaling = 1.0 / L
+    filter_ones = []
     for c in range(4):
         part = slice(L * c, L * (c + 1))
         gated_one = (back_two[:, part] * gates[c]).astype(BF16)
@@ -287,11 +301,13 @@
         pairs = jnp.where(lane_index >= L - 1 - row_index, now, then)
         turned = pltpu.roll(pairs, 1, 1, stride=1, stride_axis=0)
         filter_one = jnp.sum(turned, axis=0, keepdims=True) * scaling
-        rows[pl.ds(c, L, stride=16), :] = back_two[:, part]
-        rows[pl.ds(4 + c, L, stride=16), :] = long_mix[:, part]
-        rows[pl.ds(8 + c, L, stride=16), :] = filter_two[:, part] * scaling
-        rows[pl.ds(12 + c, L, stride=16), :] = jnp.broadcast_to(filter_one, (L, L))
-    out[...] = rows[0 : 16 * L, :].reshape(L, 16, L).astype(BF16)
+        filter_ones.append(jnp.broadcast_to(filter_one, (L, L)))
+    long_mix = restore(real_h * real_u - imag_h * imag_u, real_h * imag_u + imag_h * real_u)
+    early = send(half.at[0], 0, back_two, long_mix)
+    filter_two = restore(real_u * real_g + imag_u * imag_g, real_u * imag_g - imag_u * real_g)
+    late = send(half.at[1], 1, filter_two * scaling, jnp.concatenate(filter_ones, axis=1))
+    early.wait()
+    late.wait()
 
 
 def turn_kernel(arrived, sq, lk, back_out, gated_out, rows):
@@ -322,7 +338,7 @@
         mixed_grad = (back_two * lk[:, lanes].astype(F32)).astype(BF16).astype(F32)
         short_v[:, lanes] = (mixed_grad * mix).astype(BF16)
         key_v[:, lanes] = (back_two * mixed).astype(BF16)
-        query_v[:, lanes] = (grad_two[:, lanes].astype(F32) * array(1, c)).astype(BF16)
+        query_v[:, lanes] = (grad_two[lanes, :].astype(F32).T * array(1, c)).astype(BF16)
         filter_v[:, lanes] = array(2, c).astype(BF16)
         taps_v[:, lanes] = array(3, c).astype(BF16)
     copies = fetch(
@@ -350,7 +366,6 @@
 
 def body(sq, sk, sv, taps, lq, lk, lf, weight, out_grad):
     block = jax.ShapeDtypeStruct((L, 4 * L), BF16)
-    payload = jax.ShapeDtypeStruct((L, 16, L), BF16)
     vmem = pl.BlockSpec(memory_space=pltpu.VMEM)
     smem = pl.BlockSpec(memory_space=pltpu.SMEM)
     hbm = pl.BlockSpec(memory_space=pltpu.HBM)
@@ -367,31 +382,31 @@
     grads = lax.all_to_all(spread, "tp", 0, 0, tiled=True)
     sent_shape = pltpu.HBM((L, 16, L), BF16)
     half = jax.ShapeDtypeStruct((L, 8, L), BF16)
-    staged, gate, prod, weight_v = pl.pallas_call(
+    turned = jax.ShapeDtypeStruct((4 * L, L), BF16)
+    staged, gate, prod, turned_lq, weight_v = pl.pallas_call(
         stage_kernel,
-        out_shape=(sent_shape, half, block, jax.ShapeDtypeStruct((4 * L, 16 * L), BF16)),
-        in_specs=[hbm] * 6,
-        out_specs=(hbm, vmem, vmem, vmem),
+        out_shape=(sent_shape, half, block, turned, jax.ShapeDtypeStruct((4 * L, 16 * L), BF16)),
+        in_specs=[hbm] * 7,
+        out_specs=(hbm, vmem, vmem, vmem, vmem),
         scratch_shapes=[pltpu.VMEM((16 * L, L), F32), pltpu.VMEM((L, 16, L), BF16)]
-        + [tile] * 5
-        + [pltpu.SemaphoreType.DMA((7,))],
+        + [tile] * 6
+        + [pltpu.SemaphoreType.DMA((8,))],
         compiler_params=params(),
         name="stage",
-    )(*map(far, (lf, sk, sv, lk, sq, weight)))
+    )(*map(far, (lf, sk, sv, lk, sq, lq, weight)))
     before = passed_along(prod, CTX, 1)
     sent, grad_two = pl.pallas_call(
         join_kernel,
-        out_shape=(sent_shape, block),
-        in_specs=[vmem, vmem, vmem, hbm, hbm],
+        out_shape=(sent_shape, turned),
+        in_specs=[vmem, vmem, vmem, vmem, hbm],
         out_specs=(hbm, vmem),
         input_output_aliases={4: 0},
         scratch_shapes=[
-            pltpu.VMEM((8 * L, L), F32), tile, pltpu.VMEM((L, 8, L), BF16),
-            pltpu.SemaphoreType.DMA((2,)),
+            pltpu.VMEM((8 * L, L), F32), pltpu.VMEM((L, 8, L), BF16), pltpu.SemaphoreType.DMA,
         ],
         compiler_params=params(),
         name="join",
-    )(grads, gate, weight_v, far(lq), staged)
+    )(grads, gate, weight_v, turned_lq, staged)
     arrived = lax.all_to_all(sent, CTX, 0, 0, tiled=True)
     constants = [jnp.asarray(t) for t in tables()]
     loaded = pl.pallas_call(
@@ -416,9 +431,13 @@
     place = lax.axis_index(CTX).astype(jnp.int32).reshape(1)
     returned = pl.pallas_call(
         spectral_kernel,
-        out_shape=payload,
+        out_shape=sent_shape,
         in_specs=[smem] + [vmem] * 9,
-        scratch_shapes=[pltpu.VMEM((16 * L + 16, L), F32)],
+        out_specs=hbm,
+        scratch_shapes=[
+            pltpu.VMEM((16 * L + 16, L), F32), pltpu.VMEM((2, 8 * L, L), F32),
+            pltpu.VMEM((2, L, 8, L), BF16), pltpu.SemaphoreType.DMA((2,)),
+        ],
         compiler_params=params(),
         name="spectral",
     )(place, arrived, taps, *loaded)

time: 127 us -> 126 us (level)
  no operation moved by 1% of the time
where the time goes in v2:
time: 126 us; the launch traced here: 125 us
  waiting for transfers between devices  68.4 us (54%)
  starting transfers between devices  38 us (30%)
  Pallas kernels  18.2 us (14%)
    all_to_all x1, waiting for transfers between devices, body(): arrived = lax.all_to_all(sent, CTX, 0, 0, tiled=True)  31.5 us
    all_to_all x1, waiting for transfers between devices, body(): landed = lax.all_to_all(returned, CTX, 0, 0, tiled=True)  29.4 us
    all_to_all x1, starting transfers between devices, body(): arrived = lax.all_to_all(sent, CTX, 0, 0, tiled=True)  21.1 us
    all_to_all x1, starting transfers between devices, body(): landed = lax.all_to_all(returned, CTX, 0, 0, tiled=True)  7.32 us
    all_to_all x1, waiting for transfers between devices, body(): grads = lax.all_to_all(spread, 'tp', 0, 0, tiled=True)  5.9 us
    ppermute x2, starting transfers between devices, passed_along(): return lax.ppermute(block, axis, route)  5.55 us
    pallas_call x1, Pallas kernels, body(): pl.pallas_call(spectral_kernel, out_shape=sent_shape, in_specs=[smem] + [...  4.57 us
    all_to_all x1, starting transfers between devices, body(): grads = lax.all_to_all(spread, 'tp', 0, 0, tiled=True)  4.02 us
  transfers between devices with their start and end apart: 5, of which 4 were waited for; matrix products, arithmetic and copies ran while one was open for 0% of the time, Pallas kernels for 7%

profile of v2, /device:TPU:25, one launch (start us, length us, event | category | flops | bytes accessed | tf_op | source)
XLA Modules:
  0.0 125.4 jit_solution(10950067709071274721)
XLA Ops:
  0.6 1.7 %spread.1 = bf16[4,128,512]{2,1,0:T(8,128)(2,1)} custom-call(bf16[128,512]{1,0:T(8,128)(2,1)} %grads.1), custom_call_target="tpu_custom_call" | custom-call | tf_op jit(solution)/shard_map/spread/pallas_call | solution.py:373
  2.4 4.0 %all-to-all-start = ((bf16[4,128,512]{2,1,0:T(8,128)(2,1)}), bf16[4,128,512]{2,1,0:T(8,128)(2,1)S(1)}, u32[]{:S(2)}, u32[]{:S(2)}) async-start(bf16[4,128,512]{2,1,0:T(8,128)(2,1)} %spread.1), calls=%async_computation | async-start | bytes 1048576 | tf_op jit(solution)/shard_map/all_to_all | solution.py:382
  6.4 2.4 %stage.1 = (bf16[128,16,128]{2,1,0:T(8,128)(2,1)}, bf16[128,8,128]{2,1,0:T(8,128)(2,1)S(1)}, bf16[128,512]{1,0:T(8,128)(2,1)S(1)}, bf16[512,128]{1,0:T(8,128)(2,1)S(1)}, bf16[512,2048]{1,0:T(8,128)(2,1)S(1)}) custom-call(bf16[128,512]{1,0:T(8,128)(2,1)} %lf.1, bf16[128,512]{1,0:T(8,128)(2,1)} %sk.3, bf16[128,512]{1,0:T(8,128)(2,1)} %sv.3, ...), custom_call_target="tpu_custom_call" | custom-call | tf_op jit(solution)/shard_map/stage/pallas_call | solution.py:386
  8.8 5.9 %all-to-all-done.grads = bf16[4,128,512]{2,1,0:T(8,128)(2,1)S(1)} async-done(((bf16[4,128,512]{2,1,0:T(8,128)(2,1)}), bf16[4,128,512]{2,1,0:T(8,128)(2,1)S(1)}, u32[]{:S(2)}, u32[]{:S(2)}) %all-to-all-start) | async-done | bytes 524320 | tf_op jit(solution)/shard_map/all_to_all | solution.py:382
  14.7 0.0 copy-start
  14.7 1.5 %join.1 = (bf16[128,16,128]{2,1,0:T(8,128)(2,1)}, bf16[512,128]{1,0:T(8,128)(2,1)S(1)}) custom-call(bf16[4,128,512]{2,1,0:T(8,128)(2,1)S(1)} %all-to-all-done.grads, bf16[128,8,128]{2,1,0:T(8,128)(2,1)S(1)} %get-tuple-element.31.gate, bf16[512,2048]{1,0:T(8,128)(2,1)S(1)} %get-tuple-element.32.weight, ...), custom_call_target="tpu_custom_call", output_to_operand_aliasing={{0}: (4, {})} | custom-call | tf_op jit(solution)/shard_map/join/pallas_call | solution.py:398
  16.2 0.0 copy-start.1
  16.2 0.0 copy-start.2
  16.2 21.1 %all-to-all-start.1 = ((bf16[128,16,128]{2,1,0:T(8,128)(2,1)}), bf16[128,16,128]{2,1,0:T(8,128)(2,1)S(1)}, u32[]{:S(2)}, u32[]{:S(2)}) async-start(bf16[128,16,128]{2,1,0:T(8,128)(2,1)} %get-tuple-element.35), calls=%async_computation.1 | async-start | bytes 1048576 | tf_op jit(solution)/shard_map/all_to_all | solution.py:410
  37.4 1.2 load.1
  38.6 31.5 %all-to-all-done.1.arrived = bf16[128,16,128]{2,1,0:T(8,128)(2,1)S(1)} async-done(((bf16[128,16,128]{2,1,0:T(8,128)(2,1)}), bf16[128,16,128]{2,1,0:T(8,128)(2,1)S(1)}, u32[]{:S(2)}, u32[]{:S(2)}) %all-to-all-start.1) | async-done | bytes 524320 | tf_op jit(solution)/shard_map/all_to_all | solution.py:410
  70.1 0.0 copy-done
  70.1 4.6 %spectral.1 = bf16[128,16,128]{2,1,0:T(8,128)(2,1)} custom-call(s32[1]{0:T(128)} %bitcast.place, bf16[128,16,128]{2,1,0:T(8,128)(2,1)S(1)} %all-to-all-done.1.arrived, bf16[128,512]{1,0:T(8,128)(2,1)S(1)} %copy-done, bf16[256,256]{1,0:T(8,128)(2,1)S(1)} %get-tuple-element.36.forward, bf16[256,256]{1,0:T(8,128)(2,1)S(1)} %get-tuple-element.37.high_ref, ...), custom_call_target="tpu_custom_call" | custom-call | tf_op jit(solution)/shard_map/spectral/pallas_call | solution.py:432
  74.7 0.0 copy-start.3
  74.7 0.0 copy-start.4
  74.7 7.3 %all-to-all-start.2 = ((bf16[128,16,128]{2,1,0:T(8,128)(2,1)}), bf16[128,16,128]{2,1,0:T(8,128)(2,1)S(1)}, u32[]{:S(2)}, u32[]{:S(2)}) async-start(bf16[128,16,128]{2,1,0:T(8,128)(2,1)} %spectral.1), calls=%async_computation.2 | async-start | bytes 1048576 | tf_op jit(solution)/shard_map/all_to_all | solution.py:444
  82.0 3.4 %collective-permute-start = (bf16[128,512]{1,0:T(8,128)(2,1)S(1)}, bf16[128,512]{1,0:T(8,128)(2,1)S(1)}, u32[]{:S(2)}, u32[]{:S(2)}) collective-permute-start(bf16[128,512]{1,0:T(8,128)(2,1)S(1)} %get-tuple-element.46.prod), channel_id=1, source_target_pairs={{0,4},{4,8},{8,12},{12,16},{16,20},{20,24},{24,28},{28,32},{32,36}... | collective-permute-start | bytes 393224 | tf_op jit(solution)/shard_map/ppermute | solution.py:364
  85.4 29.4 %all-to-all-done.2.arrived = bf16[128,16,128]{2,1,0:T(8,128)(2,1)S(1)} async-done(((bf16[128,16,128]{2,1,0:T(8,128)(2,1)}), bf16[128,16,128]{2,1,0:T(8,128)(2,1)S(1)}, u32[]{:S(2)}, u32[]{:S(2)}) %all-to-all-start.2) | async-done | bytes 524320 | tf_op jit(solution)/shard_map/all_to_all | solution.py:444
  114.8 0.0 copy-done.1
  114.8 0.0 copy-done.2
  114.8 0.2 turn.1
  115.0 2.2 %collective-permute-start.1 = (bf16[128,512]{1,0:T(8,128)(2,1)S(1)}, bf16[128,512]{1,0:T(8,128)(2,1)S(1)}, u32[]{:S(2)}, u32[]{:S(2)}) collective-permute-start(bf16[128,512]{1,0:T(8,128)(2,1)S(1)} %get-tuple-element.44.gated), channel_id=1, source_target_pairs={{4,0},{8,4},{12,8},{16,12},{20,16},{24,20},{28,24},{32,28},{36,32}... | collective-permute-start | bytes 393224 | tf_op jit(solution)/shard_map/ppermute | solution.py:364
  117.1 0.0 collective-permute-done.before
  117.2 2.7 %mix.1.short_mix = f32[128,512]{1,0:T(8,128)S(1)} custom-call(bf16[128,512]{1,0:T(8,128)(2,1)S(1)} %collective-permute-done.before, bf16[128,512]{1,0:T(8,128)(2,1)S(1)} %get-tuple-element.46.prod, bf16[128,512]{1,0:T(8,128)(2,1)S(1)} %copy-done), custom_call_target="tpu_custom_call" | custom-call | tf_op jit(solution)/shard_map/mix/pallas_call | solution.py:424
  119.8 1.9 %post.1 = (bf16[128,512]{1,0:T(8,128)(2,1)}, bf16[128,512]{1,0:T(8,128)(2,1)}, bf16[128,512]{1,0:T(8,128)(2,1)}, bf16[128,512]{1,0:T(8,128)(2,1)}, bf16[128,512]{1,0:T(8,128)(2,1)}, /*index=5*/f32[128,512]{1,0:T(8,128)S(1)}) custom-call(bf16[128,16,128]{2,1,0:T(8,128)(2,1)S(1)} %all-to-all-done.2.arrived, bf16[128,512]{1,0:T(8,128)(2,1)S(1)} %get-tuple-element.43.back, ...), custom_call_target="tpu_custom_call" | custom-call | tf_op jit(solution)/shard_map/post/pallas_call | solution.py:458
  121.7 1.6 %collective-permute-done.1.after = bf16[128,512]{1,0:T(8,128)(2,1)S(1)} collective-permute-done((bf16[128,512]{1,0:T(8,128)(2,1)S(1)}, bf16[128,512]{1,0:T(8,128)(2,1)S(1)}, u32[]{:S(2)}, u32[]{:S(2)}) %collective-permute-start.1) | collective-permute-done | bytes 131104 | tf_op jit(solution)/shard_map/ppermute | solution.py:364
  123.4 0.0 copy-done.3
  123.4 0.0 copy-done.4
  123.4 2.1 %last.1 = (bf16[128,512]{1,0:T(8,128)(2,1)}, bf16[128,512]{1,0:T(8,128)(2,1)}) custom-call(bf16[128,512]{1,0:T(8,128)(2,1)S(1)} %collective-permute-done.1.after, f32[128,512]{1,0:T(8,128)S(1)} %get-tuple-element.48.partial, bf16[128,512]{1,0:T(8,128)(2,1)S(1)} %copy-done, bf16[128,512]{1,0:T(8,128)(2,1)S(1)} %copy-done.3, bf16[128,512]{1,0:T(8,128)(2,1)S(1)} %copy-done.4), custom_call_target="tpu_custom_call" | custom-call | tf_op jit(solution)/shard_map/last/pallas_call | solution.py:466
Async XLA Ops:
  2.4 12.4 %all-to-all-start = ((bf16[4,128,512]{2,1,0:T(8,128)(2,1)}), bf16[4,128,512]{2,1,0:T(8,128)(2,1)S(1)}, u32[]{:S(2)}, u32[]{:S(2)}) async-start(bf16[4,128,512]{2,1,0:T(8,128)(2,1)} %spread.1), calls=%async_computation | async-start | bytes 1048576 | tf_op jit(solution)/shard_map/all_to_all | solution.py:382
  14.7 55.4 %copy-start = (bf16[128,512]{1,0:T(8,128)(2,1)S(1)}, bf16[128,512]{1,0:T(8,128)(2,1)}, u32[]{:S(2)}) copy-start(bf16[128,512]{1,0:T(8,128)(2,1)} %taps_in.7) | copy-start | bytes 393220
  16.2 98.6 %copy-start.1 = (bf16[128,512]{1,0:T(8,128)(2,1)S(1)}, bf16[128,512]{1,0:T(8,128)(2,1)}, u32[]{:S(2)}) copy-start(bf16[128,512]{1,0:T(8,128)(2,1)} %lk.5) | copy-start | bytes 393220
  16.2 98.6 %copy-start.2 = (bf16[128,512]{1,0:T(8,128)(2,1)S(1)}, bf16[128,512]{1,0:T(8,128)(2,1)}, u32[]{:S(2)}) copy-start(bf16[128,512]{1,0:T(8,128)(2,1)} %sq.5) | copy-start | bytes 393220
  16.2 53.9 %all-to-all-start.1 = ((bf16[128,16,128]{2,1,0:T(8,128)(2,1)}), bf16[128,16,128]{2,1,0:T(8,128)(2,1)S(1)}, u32[]{:S(2)}, u32[]{:S(2)}) async-start(bf16[128,16,128]{2,1,0:T(8,128)(2,1)} %get-tuple-element.35), calls=%async_computation.1 | async-start | bytes 1048576 | tf_op jit(solution)/shard_map/all_to_all | solution.py:410
  74.7 48.7 %copy-start.3 = (bf16[128,512]{1,0:T(8,128)(2,1)S(1)}, bf16[128,512]{1,0:T(8,128)(2,1)}, u32[]{:S(2)}) copy-start(bf16[128,512]{1,0:T(8,128)(2,1)} %sk.3) | copy-start | bytes 393220
  74.7 48.7 %copy-start.4 = (bf16[128,512]{1,0:T(8,128)(2,1)S(1)}, bf16[128,512]{1,0:T(8,128)(2,1)}, u32[]{:S(2)}) copy-start(bf16[128,512]{1,0:T(8,128)(2,1)} %sv.3) | copy-start | bytes 393220
  74.7 40.1 %all-to-all-start.2 = ((bf16[128,16,128]{2,1,0:T(8,128)(2,1)}), bf16[128,16,128]{2,1,0:T(8,128)(2,1)S(1)}, u32[]{:S(2)}, u32[]{:S(2)}) async-start(bf16[128,16,128]{2,1,0:T(8,128)(2,1)} %spectral.1), calls=%async_computation.2 | async-start | bytes 1048576 | tf_op jit(solution)/shard_map/all_to_all | solution.py:444
  82.0 35.1 %collective-permute-start = (bf16[128,512]{1,0:T(8,128)(2,1)S(1)}, bf16[128,512]{1,0:T(8,128)(2,1)S(1)}, u32[]{:S(2)}, u32[]{:S(2)}) collective-permute-start(bf16[128,512]{1,0:T(8,128)(2,1)S(1)} %get-tuple-element.46.prod), channel_id=1, source_target_pairs={{0,4},{4,8},{8,12},{12,16},{16,20},{20,24},{24,28},{28,32},{32,36}... | collective-permute-start | bytes 393224 | tf_op jit(solution)/shard_map/ppermute | solution.py:364
  115.0 8.4 %collective-permute-start.1 = (bf16[128,512]{1,0:T(8,128)(2,1)S(1)}, bf16[128,512]{1,0:T(8,128)(2,1)S(1)}, u32[]{:S(2)}, u32[]{:S(2)}) collective-permute-start(bf16[128,512]{1,0:T(8,128)(2,1)S(1)} %get-tuple-element.44.gated), channel_id=1, source_target_pairs={{4,0},{8,4},{12,8},{16,12},{20,16},{24,20},{28,24},{32,28},{36,32}... | collective-permute-start | bytes 393224 | tf_op jit(solution)/shard_map/ppermute | solution.py:364

commit v3 on v2

--- a/solution.py
+++ b/solution.py
@@ -165,48 +165,6 @@
     mix_loop(ext, taps, shifted, finish)
 
 
-def back_loop(ext, taps, shifted, inside, finish):
-    def chunk(index, carry):
-        lanes = pl.ds(pl.multiple_of(index * L, L), L)
-        total = [jnp.zeros((8, L), F32) for _ in range(16)]
-        for shift in range(8):
-            shifted[...] = ext[shift : L + shift, lanes]
-            for group in range(16):
-                tap = taps[8 * group + shift : 8 * group + shift + 1, lanes]
-                for tile in range(16 - group if inside else group + 1):
-                    source = tile + group if inside else tile
-                    place = tile if inside else 15 - group + tile
-                    total[place] += tap * shifted[8 * source : 8 * (source + 1), :]
-        finish(lanes, jnp.concatenate(total, axis=0), index)
-        return carry
-
-    lax.fori_loop(0, 4, chunk, 0)
-
-
-def last_kernel(after, partial, taps_in, sk, sv, key_out, value_out, ext, taps, shifted, key_v, value_v, marks):
-    ext[0:8, :] = jnp.zeros((8, 4 * L), F32)
-    ext[8:, :] = after[...].astype(F32)
-    taps[...] = taps_in[...].astype(F32)
-
-    def outward(lanes, index):
-        return (
-            pltpu.make_async_copy(key_v.at[:, lanes], key_out.at[:, lanes], marks.at[0, index]),
-            pltpu.make_async_copy(value_v.at[:, lanes], value_out.at[:, lanes], marks.at[1, index]),
-        )
-
-    def finish(lanes, total, index):
-        total += partial[:, lanes]
-        key_v[:, lanes] = (total * sv[:, lanes].astype(F32)).astype(BF16)
-        value_v[:, lanes] = (total * sk[:, lanes].astype(F32)).astype(BF16)
-        for copy in outward(lanes, index):
-            copy.start()
-
-    back_loop(ext, taps, shifted, False, finish)
-    for index in range(4):
-        for copy in outward(pl.ds(L * index, L), index):
-            copy.wait()
-
-
 def load_kernel(*refs):
     count = len(refs) // 2
     for copy in fetch(refs[:count], refs[count : 2 * count], refs[-1]):
@@ -215,7 +173,7 @@
 
 def spectral_kernel(
     place, arrived, taps_in, forward, high_ref, low_ref, cos_ref, sin_ref, back_high, back_low,
-    out, rows, half, out_v, marks,
+    out, rows, sent, out_v, marks,
 ):
     rows[0:16, :] = jnp.zeros((16, L), F32)
     rows[16:, :] = arrived[...].astype(F32).reshape(16 * L, L)
@@ -227,7 +185,8 @@
     lane_index = lax.broadcasted_iota(jnp.int32, (L, L), 1)
     chosen = (lax.broadcasted_iota(jnp.int32, (16, L), 1) == place[0]).astype(F32).astype(BF16)
     flip = (row_index + lane_index == L - 1).astype(F32).astype(BF16)
-    prods, earlier, gates = [], [], []
+    onward = (lane_index == row_index + 1).astype(F32).astype(BF16)
+    prods, earlier, gates, owns, others = [], [], [], [], []
     product_two = []
     for c in range(4):
         prods.append(array(1, c).astype(BF16))
@@ -237,6 +196,8 @@
         turned = pltpu.roll(jnp.broadcast_to(taps, (L, L)), 0, 1, stride=1, stride_axis=0)
         own = jnp.where(lane_index >= row_index, turned, 0.0).astype(BF16)
         other = jnp.where(lane_index < row_index, turned, 0.0).astype(BF16)
+        owns.append(own)
+        others.append(other)
         short_mix = nn(prods[c], own) + nn(earlier[c], other)
         product_two.append((gates[c] * short_mix).astype(BF16))
 
@@ -278,21 +239,11 @@
     real_g, imag_g = spectrum([array(3, c).astype(BF16) for c in range(4)])
     real_u, imag_u = spectrum(product_two)
 
-    def send(half, group, first, second):
-        for c in range(4):
-            part = slice(L * c, L * (c + 1))
-            half[pl.ds(c, L, stride=8), :] = first[:, part]
-            half[pl.ds(4 + c, L, stride=8), :] = second[:, part]
-        out_v[group] = half[...].reshape(L, 8, L).astype(BF16)
-        copy = pltpu.make_async_copy(
-            out_v.at[group], out.at[:, 8 * group : 8 * (group + 1), :], marks.at[group]
-        )
-        copy.start()
-        return copy
+    def store(a, c, value):
+        sent[pl.ds(4 * a + c, L, stride=20), :] = value
 
     scaling = 1.0 / L
     back_two = restore(real_h * real_g + imag_h * imag_g, real_h * imag_g - imag_h * real_g)
-    filter_ones = []
     for c in range(4):
         part = slice(L * c, L * (c + 1))
         gated_one = (back_two[:, part] * gates[c]).astype(BF16)
@@ -301,59 +252,60 @@
         pairs = jnp.where(lane_index >= L - 1 - row_index, now, then)
         turned = pltpu.roll(pairs, 1, 1, stride=1, stride_axis=0)
         filter_one = jnp.sum(turned, axis=0, keepdims=True) * scaling
-        filter_ones.append(jnp.broadcast_to(filter_one, (L, L)))
+        later = nn(onward, gated_one).astype(BF16)
+        store(0, c, back_two[:, part])
+        store(3, c, jnp.broadcast_to(filter_one, (L, L)))
+        store(4, c, nt(gated_one, owns[c]) + nt(later, others[c]))
     long_mix = restore(real_h * real_u - imag_h * imag_u, real_h * imag_u + imag_h * real_u)
-    early = send(half.at[0], 0, back_two, long_mix)
+    for c in range(4):
+        store(1, c, long_mix[:, L * c : L * (c + 1)])
     filter_two = restore(real_u * real_g + imag_u * imag_g, real_u * imag_g - imag_u * real_g)
-    late = send(half.at[1], 1, filter_two * scaling, jnp.concatenate(filter_ones, axis=1))
-    early.wait()
-    late.wait()
-
-
-def turn_kernel(arrived, sq, lk, back_out, gated_out, rows):
-    rows[...] = arrived[...].astype(F32).reshape(16 * L, L)
+    for c in range(4):
+        store(2, c, filter_two[:, L * c : L * (c + 1)] * scaling)
+    copies = []
+    for k in range(4):
+        part = pl.ds(5 * L * k, 5 * L)
+        out_v[part, :] = sent[part, :].astype(BF16)
+        copies.append(pltpu.make_async_copy(out_v.at[part, :], out.at[part, :], marks.at[k]))
+        copies[k].start()
+    for copy in copies:
+        copy.wait()
+
+
+def post_kernel(
+    arrived, grad_two, short_mix, sq, lk, sk, sv, short_out, key_one_out, value_one_out, taps_out,
+    query_out, key_out, filter_out, rows, results, marks,
+):
+    rows[...] = arrived[...].astype(F32)
+    outs = (short_out, key_one_out, value_one_out, taps_out, query_out, key_out, filter_out)
+    copies = []
+
+    def array(a, c):
+        return rows[pl.ds(4 * a + c, L, stride=20), :].T
+
     for c in range(4):
         lanes = slice(L * c, L * (c + 1))
-        back_two = rows[pl.ds(c, L, stride=16), :].T
-        back_out[:, lanes] = back_two.astype(BF16)
-        mixed_grad = (back_two * lk[:, lanes].astype(F32)).astype(BF16).astype(F32)
-        gated_out[:, lanes] = (mixed_grad * sq[:, lanes].astype(F32)).astype(BF16)
-
-
-def post_kernel(
-    arrived, back, gated, grad_two, short_mix, sq, lk, taps_in, query_out, key_out, filter_out,
-    taps_out, short_out, partial, rows, ext, taps, shifted, query_v, key_v, filter_v, taps_v,
-    short_v, marks,
-):
-    rows[...] = arrived[...].astype(F32).reshape(16 * L, L)
-
-    def array(a, c):
-        return rows[pl.ds(4 * a + c, L, stride=16), :].T
-
-    for c in range(4):
-        lanes = slice(L * c, L * (c + 1))
-        back_two = back[:, lanes].astype(F32)
+        back_two, back_one = array(0, c), array(4, c)
         mix = short_mix[:, lanes]
         mixed = (sq[:, lanes].astype(F32) * mix).astype(BF16).astype(F32)
         mixed_grad = (back_two * lk[:, lanes].astype(F32)).astype(BF16).astype(F32)
-        short_v[:, lanes] = (mixed_grad * mix).astype(BF16)
-        key_v[:, lanes] = (back_two * mixed).astype(BF16)
-        query_v[:, lanes] = (grad_two[lanes, :].astype(F32).T * array(1, c)).astype(BF16)
-        filter_v[:, lanes] = array(2, c).astype(BF16)
-        taps_v[:, lanes] = array(3, c).astype(BF16)
-    copies = fetch(
-        (query_v, key_v, filter_v, taps_v, short_v),
-        (query_out, key_out, filter_out, taps_out, short_out),
-        marks,
-    )
-    ext[0:L, :] = gated[...].astype(F32)
-    ext[L:, :] = jnp.zeros((8, 4 * L), F32)
-    taps[...] = taps_in[...].astype(F32)
-
-    def finish(lanes, total, index):
-        partial[:, lanes] = total
-
-    back_loop(ext, taps, shifted, True, finish)
+        values = (
+            mixed_grad * mix,
+            back_one * sv[:, lanes].astype(F32),
+            back_one * sk[:, lanes].astype(F32),
+            array(3, c),
+            grad_two[lanes, :].astype(F32).T * array(1, c),
+            back_two * mixed,
+            array(2, c),
+        )
+        for k, value in enumerate(values):
+            results[k, :, lanes] = value.astype(BF16)
+            copies.append(
+                pltpu.make_async_copy(
+                    results.at[k, :, lanes], outs[k].at[:, lanes], marks.at[k, c]
+                )
+            )
+            copies[-1].start()
     for copy in copies:
         copy.wait()
 
@@ -431,49 +383,29 @@
     place = lax.axis_index(CTX).astype(jnp.int32).reshape(1)
     returned = pl.pallas_call(
         spectral_kernel,
-        out_shape=sent_shape,
+        out_shape=pltpu.HBM((20 * L, L), BF16),
         in_specs=[smem] + [vmem] * 9,
         out_specs=hbm,
         scratch_shapes=[
-            pltpu.VMEM((16 * L + 16, L), F32), pltpu.VMEM((2, 8 * L, L), F32),
-            pltpu.VMEM((2, L, 8, L), BF16), pltpu.SemaphoreType.DMA((2,)),
+            pltpu.VMEM((16 * L + 16, L), F32), pltpu.VMEM((20 * L, L), F32),
+            pltpu.VMEM((20 * L, L), BF16), pltpu.SemaphoreType.DMA((4,)),
         ],
         compiler_params=params(),
         name="spectral",
     )(place, arrived, taps, *loaded)
-    landed = lax.all_to_all(returned, CTX, 0, 0, tiled=True)
-    landed_rows = pltpu.VMEM((16 * L, L), F32)
-    back, gated = pl.pallas_call(
-        turn_kernel,
-        out_shape=(block, block),
-        scratch_shapes=[landed_rows],
-        compiler_params=params(),
-        name="turn",
-    )(landed, sq, lk)
-    after = passed_along(gated, CTX, -1)
-    back_scratch = [
-        pltpu.VMEM((L + 8, 4 * L), F32), pltpu.VMEM((L, 4 * L), F32), pltpu.VMEM((L, L), F32)
-    ]
-    out_block = pltpu.HBM((L, 4 * L), BF16)
-    query_out, key_out, filter_out, taps_out, short_out, partial = pl.pallas_call(
+    returned = returned.reshape(L, 5, 4, L)
+    landed = lax.all_to_all(returned, CTX, 0, 0, tiled=True).reshape(20 * L, L)
+    return pl.pallas_call(
         post_kernel,
-        out_shape=(out_block,) * 5 + (jax.ShapeDtypeStruct((L, 4 * L), F32),),
-        out_specs=(hbm,) * 5 + (vmem,),
-        scratch_shapes=[landed_rows] + back_scratch + [tile] * 5 + [pltpu.SemaphoreType.DMA((5,))],
+        out_shape=(pltpu.HBM((L, 4 * L), BF16),) * 7,
+        out_specs=(hbm,) * 7,
+        scratch_shapes=[
+            pltpu.VMEM((20 * L, L), F32), pltpu.VMEM((7, L, 4 * L), BF16),
+            pltpu.SemaphoreType.DMA((7, 4)),
+        ],
         compiler_params=params(),
         name="post",
-    )(landed, back, gated, grad_two, short_mix, sq, lk, taps)
-    short_key_grad, short_value_grad = pl.pallas_call(
-        last_kernel,
-        out_shape=(out_block,) * 2,
-        out_specs=(hbm,) * 2,
-        scratch_shapes=back_scratch + [tile] * 2 + [pltpu.SemaphoreType.DMA((2, 4))],
-        compiler_params=params(),
-        name="last",
-    )(after, partial, taps, sk, sv)
-    return (
-        short_out, short_key_grad, short_value_grad, taps_out, query_out, key_out, filter_out
-    )
+    )(landed, grad_two, short_mix, sq, lk, sk, sv)
 
 
 def solution(mesh):

time: 126 us -> 123 us (0.976)
  starting transfers between devices: 38 us -> 35.6 us
  Pallas kernels: 18.2 us -> 16.2 us
    ppermute x2 -> x1, waiting for transfers between devices: 1.64 us -> 22.3 us  [passed_along(): return lax.ppermute(block, axis, route)]
    all_to_all x1, waiting for transfers between devices: 29.4 us -> 9.86 us  [body(): landed = lax.all_to_all(returned, CTX, 0, 0, tiled=True).reshape(20 * L, L)]
    ppermute x2 -> x1, starting transfers between devices: 5.55 us -> 3.37 us  [passed_along(): return lax.ppermute(block, axis, route)]
    pallas_call x4 -> x2, Pallas kernels: 8.71 us -> 6.72 us  [the longest x1 5.31 us: body(): pl.pallas_call(spectral_kernel, out_shape=pltpu.HBM((20 * L, L), BF16), i...]
  transfers between devices with their start and end apart: 5 -> 4, of which waited for: 4 -> 4; matrix products, arithmetic and copies ran while one was open for 0% -> 0% of each run, Pallas kernels for 7% -> 5%
where the time goes in v3:
time: 123 us; the launch traced here: 122 us
  waiting for transfers between devices  69.5 us (57%)
  starting transfers between devices  35.6 us (29%)
  Pallas kernels  16.2 us (13%)
    all_to_all x1, waiting for transfers between devices, body(): arrived = lax.all_to_all(sent, CTX, 0, 0, tiled=True)  31.5 us
    ppermute x1, waiting for transfers between devices, passed_along(): return lax.ppermute(block, axis, route)  22.3 us
    all_to_all x1, starting transfers between devices, body(): arrived = lax.all_to_all(sent, CTX, 0, 0, tiled=True)  21 us
    all_to_all x1, waiting for transfers between devices, body(): landed = lax.all_to_all(returned, CTX, 0, 0, tiled=True).reshape(20 * L, L)  9.86 us
    all_to_all x1, starting transfers between devices, body(): landed = lax.all_to_all(returned, CTX, 0, 0, tiled=True).reshape(20 * L, L)  7.19 us
    all_to_all x1, waiting for transfers between devices, body(): grads = lax.all_to_all(spread, 'tp', 0, 0, tiled=True)  5.91 us
    pallas_call x1, Pallas kernels, body(): pl.pallas_call(spectral_kernel, out_shape=pltpu.HBM((20 * L, L), BF16), i...  5.31 us
    all_to_all x1, starting transfers between devices, body(): grads = lax.all_to_all(spread, 'tp', 0, 0, tiled=True)  4.02 us
  transfers between devices with their start and end apart: 4, of which 4 were waited for; matrix products, arithmetic and copies ran while one was open for 0% of the time, Pallas kernels for 5%

profile of v3, /device:TPU:25, one launch (start us, length us, event | category | flops | bytes accessed | tf_op | source)
XLA Modules:
  0.0 122.1 jit_solution(11851986341579687982)
XLA Ops:
  0.6 1.7 %spread.1 = bf16[4,128,512]{2,1,0:T(8,128)(2,1)} custom-call(bf16[128,512]{1,0:T(8,128)(2,1)} %grads.1), custom_call_target="tpu_custom_call" | custom-call | tf_op jit(solution)/shard_map/spread/pallas_call | solution.py:325
  2.4 4.0 %all-to-all-start = ((bf16[4,128,512]{2,1,0:T(8,128)(2,1)}), bf16[4,128,512]{2,1,0:T(8,128)(2,1)S(1)}, u32[]{:S(2)}, u32[]{:S(2)}) async-start(bf16[4,128,512]{2,1,0:T(8,128)(2,1)} %spread.1), calls=%async_computation | async-start | bytes 1048576 | tf_op jit(solution)/shard_map/all_to_all | solution.py:334
  6.4 2.4 %stage.1 = (bf16[128,16,128]{2,1,0:T(8,128)(2,1)}, bf16[128,8,128]{2,1,0:T(8,128)(2,1)S(1)}, bf16[128,512]{1,0:T(8,128)(2,1)S(1)}, bf16[512,128]{1,0:T(8,128)(2,1)S(1)}, bf16[512,2048]{1,0:T(8,128)(2,1)S(1)}) custom-call(bf16[128,512]{1,0:T(8,128)(2,1)} %lf.1, bf16[128,512]{1,0:T(8,128)(2,1)} %sk.3, bf16[128,512]{1,0:T(8,128)(2,1)} %sv.3, ...), custom_call_target="tpu_custom_call" | custom-call | tf_op jit(solution)/shard_map/stage/pallas_call | solution.py:338
  8.8 5.9 %all-to-all-done.grads = bf16[4,128,512]{2,1,0:T(8,128)(2,1)S(1)} async-done(((bf16[4,128,512]{2,1,0:T(8,128)(2,1)}), bf16[4,128,512]{2,1,0:T(8,128)(2,1)S(1)}, u32[]{:S(2)}, u32[]{:S(2)}) %all-to-all-start) | async-done | bytes 524320 | tf_op jit(solution)/shard_map/all_to_all | solution.py:334
  14.7 0.0 copy-start
  14.7 1.5 %join.1 = (bf16[128,16,128]{2,1,0:T(8,128)(2,1)}, bf16[512,128]{1,0:T(8,128)(2,1)S(1)}) custom-call(bf16[4,128,512]{2,1,0:T(8,128)(2,1)S(1)} %all-to-all-done.grads, bf16[128,8,128]{2,1,0:T(8,128)(2,1)S(1)} %get-tuple-element.21.gate, bf16[512,2048]{1,0:T(8,128)(2,1)S(1)} %get-tuple-element.22.weight, ...), custom_call_target="tpu_custom_call", output_to_operand_aliasing={{0}: (4, {})} | custom-call | tf_op jit(solution)/shard_map/join/pallas_call | solution.py:350
  16.2 21.0 %all-to-all-start.1 = ((bf16[128,16,128]{2,1,0:T(8,128)(2,1)}), bf16[128,16,128]{2,1,0:T(8,128)(2,1)S(1)}, u32[]{:S(2)}, u32[]{:S(2)}) async-start(bf16[128,16,128]{2,1,0:T(8,128)(2,1)} %get-tuple-element.25), calls=%async_computation.1 | async-start | bytes 1048576 | tf_op jit(solution)/shard_map/all_to_all | solution.py:362
  37.2 1.2 load.1
  38.4 0.0 copy-start.1
  38.4 0.0 copy-start.2
  38.4 0.0 copy-start.3
  38.5 0.0 copy-start.4
  38.5 31.5 %all-to-all-done.1.arrived = bf16[128,16,128]{2,1,0:T(8,128)(2,1)S(1)} async-done(((bf16[128,16,128]{2,1,0:T(8,128)(2,1)}), bf16[128,16,128]{2,1,0:T(8,128)(2,1)S(1)}, u32[]{:S(2)}, u32[]{:S(2)}) %all-to-all-start.1) | async-done | bytes 524320 | tf_op jit(solution)/shard_map/all_to_all | solution.py:362
  70.0 0.0 copy-done
  70.0 5.3 %spectral.1 = bf16[2560,128]{1,0:T(8,128)(2,1)} custom-call(s32[1]{0:T(128)} %bitcast.place, bf16[128,16,128]{2,1,0:T(8,128)(2,1)S(1)} %all-to-all-done.1.arrived, bf16[128,512]{1,0:T(8,128)(2,1)S(1)} %copy-done, bf16[256,256]{1,0:T(8,128)(2,1)S(1)} %get-tuple-element.26.forward, bf16[256,256]{1,0:T(8,128)(2,1)S(1)} %get-tuple-element.27.high_ref, ...), custom_call_target="tpu_custom_call" | custom-call | tf_op jit(solution)/shard_map/spectral/pallas_call | solution.py:384
  75.3 7.2 %all-to-all-start.2 = ((bf16[128,5,4,128]{3,2,1,0:T(4,128)(2,1)}), bf16[128,5,4,128]{3,2,1,0:T(4,128)(2,1)S(1)}, u32[]{:S(2)}, u32[]{:S(2)}) async-start(bf16[128,5,4,128]{3,2,1,0:T(4,128)(2,1)} %bitcast.4), calls=%async_computation.2 | async-start | bytes 1310720 | tf_op jit(solution)/shard_map/all_to_all | solution.py:397
  82.5 3.4 %collective-permute-start = (bf16[128,512]{1,0:T(8,128)(2,1)S(1)}, bf16[128,512]{1,0:T(8,128)(2,1)S(1)}, u32[]{:S(2)}, u32[]{:S(2)}) collective-permute-start(bf16[128,512]{1,0:T(8,128)(2,1)S(1)} %get-tuple-element.34.prod), channel_id=1, source_target_pairs={{0,4},{4,8},{8,12},{12,16},{16,20},{20,24},{24,28},{28,32},{32,36}... | collective-permute-start | bytes 393224 | tf_op jit(solution)/shard_map/ppermute | solution.py:316
  85.9 22.3 %collective-permute-done.before = bf16[128,512]{1,0:T(8,128)(2,1)S(1)} collective-permute-done((bf16[128,512]{1,0:T(8,128)(2,1)S(1)}, bf16[128,512]{1,0:T(8,128)(2,1)S(1)}, u32[]{:S(2)}, u32[]{:S(2)}) %collective-permute-start) | collective-permute-done | bytes 131104 | tf_op jit(solution)/shard_map/ppermute | solution.py:316
  108.1 2.7 %mix.1.short_mix = f32[128,512]{1,0:T(8,128)S(1)} custom-call(bf16[128,512]{1,0:T(8,128)(2,1)S(1)} %collective-permute-done.before, bf16[128,512]{1,0:T(8,128)(2,1)S(1)} %get-tuple-element.34.prod, bf16[128,512]{1,0:T(8,128)(2,1)S(1)} %copy-done), custom_call_target="tpu_custom_call" | custom-call | tf_op jit(solution)/shard_map/mix/pallas_call | solution.py:376
  110.8 9.9 %all-to-all-done.2 = bf16[128,5,4,128]{3,2,1,0:T(4,128)(2,1)S(1)} async-done(((bf16[128,5,4,128]{3,2,1,0:T(4,128)(2,1)}), bf16[128,5,4,128]{3,2,1,0:T(4,128)(2,1)S(1)}, u32[]{:S(2)}, u32[]{:S(2)}) %all-to-all-start.2) | async-done | bytes 655392 | tf_op jit(solution)/shard_map/all_to_all | solution.py:397
  120.7 0.0 copy-done.1
  120.7 0.0 copy-done.2
  120.7 0.0 copy-done.3
  120.7 0.0 copy-done.4
  120.7 1.4 %post.1 = (bf16[128,512]{1,0:T(8,128)(2,1)}, bf16[128,512]{1,0:T(8,128)(2,1)}, bf16[128,512]{1,0:T(8,128)(2,1)}, bf16[128,512]{1,0:T(8,128)(2,1)}, bf16[128,512]...) custom-call(bf16[2560,128]{1,0:T(8,128)(2,1)S(1)} %bitcast.3, ...), custom_call_target="tpu_custom_call" | custom-call | tf_op jit(solution)/shard_map/post/pallas_call | solution.py:398
Async XLA Ops:
  2.4 12.4 %all-to-all-start = ((bf16[4,128,512]{2,1,0:T(8,128)(2,1)}), bf16[4,128,512]{2,1,0:T(8,128)(2,1)S(1)}, u32[]{:S(2)}, u32[]{:S(2)}) async-start(bf16[4,128,512]{2,1,0:T(8,128)(2,1)} %spread.1), calls=%async_computation | async-start | bytes 1048576 | tf_op jit(solution)/shard_map/all_to_all | solution.py:334
  14.7 55.2 %copy-start = (bf16[128,512]{1,0:T(8,128)(2,1)S(1)}, bf16[128,512]{1,0:T(8,128)(2,1)}, u32[]{:S(2)}) copy-start(bf16[128,512]{1,0:T(8,128)(2,1)} %taps_in.3) | copy-start | bytes 393220
  16.2 53.7 %all-to-all-start.1 = ((bf16[128,16,128]{2,1,0:T(8,128)(2,1)}), bf16[128,16,128]{2,1,0:T(8,128)(2,1)S(1)}, u32[]{:S(2)}, u32[]{:S(2)}) async-start(bf16[128,16,128]{2,1,0:T(8,128)(2,1)} %get-tuple-element.25), calls=%async_computation.1 | async-start | bytes 1048576 | tf_op jit(solution)/shard_map/all_to_all | solution.py:362
  38.4 82.3 %copy-start.1 = (bf16[128,512]{1,0:T(8,128)(2,1)S(1)}, bf16[128,512]{1,0:T(8,128)(2,1)}, u32[]{:S(2)}) copy-start(bf16[128,512]{1,0:T(8,128)(2,1)} %sk.3) | copy-start | bytes 393220
  38.4 82.2 %copy-start.2 = (bf16[128,512]{1,0:T(8,128)(2,1)S(1)}, bf16[128,512]{1,0:T(8,128)(2,1)}, u32[]{:S(2)}) copy-start(bf16[128,512]{1,0:T(8,128)(2,1)} %sv.3) | copy-start | bytes 393220
  38.4 82.2 %copy-start.3 = (bf16[128,512]{1,0:T(8,128)(2,1)S(1)}, bf16[128,512]{1,0:T(8,128)(2,1)}, u32[]{:S(2)}) copy-start(bf16[128,512]{1,0:T(8,128)(2,1)} %lk.3) | copy-start | bytes 393220
  38.5 82.2 %copy-start.4 = (bf16[128,512]{1,0:T(8,128)(2,1)S(1)}, bf16[128,512]{1,0:T(8,128)(2,1)}, u32[]{:S(2)}) copy-start(bf16[128,512]{1,0:T(8,128)(2,1)} %sq.3) | copy-start | bytes 393220
  75.3 45.4 %all-to-all-start.2 = ((bf16[128,5,4,128]{3,2,1,0:T(4,128)(2,1)}), bf16[128,5,4,128]{3,2,1,0:T(4,128)(2,1)S(1)}, u32[]{:S(2)}, u32[]{:S(2)}) async-start(bf16[128,5,4,128]{3,2,1,0:T(4,128)(2,1)} %bitcast.4), calls=%async_computation.2 | async-start | bytes 1310720 | tf_op jit(solution)/shard_map/all_to_all | solution.py:397
  82.5 25.7 %collective-permute-start = (bf16[128,512]{1,0:T(8,128)(2,1)S(1)}, bf16[128,512]{1,0:T(8,128)(2,1)S(1)}, u32[]{:S(2)}, u32[]{:S(2)}) collective-permute-start(bf16[128,512]{1,0:T(8,128)(2,1)S(1)} %get-tuple-element.34.prod), channel_id=1, source_target_pairs={{0,4},{4,8},{8,12},{12,16},{16,20},{20,24},{24,28},{28,32},{32,36}... | collective-permute-start | bytes 393224 | tf_op jit(solution)/shard_map/ppermute | solution.py:316

commit v4 on v3

--- a/solution.py
+++ b/solution.py
@@ -122,20 +122,24 @@
     copy.wait()
 
 
-def join_kernel(grads, gate, weight, turned_lq, staged, out, grad_two, rows, out_v, mark):
+def join_kernel(grads, gate, weight, turned_lq, staged, out, grad_two, rows, out_v, marks):
     rows[...] = gate[...].astype(F32).reshape(8 * L, L)
     total = nt(weight[:, 0:512], grads[0])
     for part in range(1, 4):
         total += nt(weight[:, 512 * part : 512 * (part + 1)], grads[part])
     grad_low = total.astype(BF16)
+    gated = grad_low.astype(F32) * turned_lq[...].astype(F32)
+    for c in range(4):
+        rows[pl.ds(4 + c, L, stride=8), :] = gated[L * c : L * (c + 1), :]
+    copies = []
+    for k in range(4):
+        part = slice(32 * k, 32 * (k + 1))
+        out_v[part] = rows[256 * k : 256 * (k + 1), :].reshape(32, 8, L).astype(BF16)
+        copies.append(pltpu.make_async_copy(out_v.at[part], out.at[part, 8:16, :], marks.at[k]))
+        copies[k].start()
     grad_two[...] = grad_low
-    gated = grad_low.astype(F32) * turned_lq[...].astype(F32)
-    for c in range(4):
-        rows[pl.ds(4 + c, L, stride=8), :] = gated[L * c : L * (c + 1), :]
-    out_v[...] = rows[...].reshape(L, 8, L).astype(BF16)
-    copy = pltpu.make_async_copy(out_v, out.at[:, 8:16, :], mark)
-    copy.start()
-    copy.wait()
+    for copy in copies:
+        copy.wait()
 
 
 def mix_loop(ext, taps, shifted, finish):
@@ -354,7 +358,7 @@
         out_specs=(hbm, vmem),
         input_output_aliases={4: 0},
         scratch_shapes=[
-            pltpu.VMEM((8 * L, L), F32), pltpu.VMEM((L, 8, L), BF16), pltpu.SemaphoreType.DMA,
+            pltpu.VMEM((8 * L, L), F32), pltpu.VMEM((L, 8, L), BF16), pltpu.SemaphoreType.DMA((4,)),
         ],
         compiler_params=params(),
         name="join",

time: 123 us -> 123 us (level)
  no operation moved by 1% of the time
where the time goes in v4:
time: 123 us; the launch traced here: 122 us
  waiting for transfers between devices  69.5 us (57%)
  starting transfers between devices  35.6 us (29%)
  Pallas kernels  16.2 us (13%)
    all_to_all x1, waiting for transfers between devices, body(): arrived = lax.all_to_all(sent, CTX, 0, 0, tiled=True)  31.5 us
    ppermute x1, waiting for transfers between devices, passed_along(): return lax.ppermute(block, axis, route)  22.3 us
    all_to_all x1, starting transfers between devices, body(): arrived = lax.all_to_all(sent, CTX, 0, 0, tiled=True)  21 us
    all_to_all x1, waiting for transfers between devices, body(): landed = lax.all_to_all(returned, CTX, 0, 0, tiled=True).reshape(20 * L, L)  9.86 us
    all_to_all x1, starting transfers between devices, body(): landed = lax.all_to_all(returned, CTX, 0, 0, tiled=True).reshape(20 * L, L)  7.19 us
    all_to_all x1, waiting for transfers between devices, body(): grads = lax.all_to_all(spread, 'tp', 0, 0, tiled=True)  5.91 us
    pallas_call x1, Pallas kernels, body(): pl.pallas_call(spectral_kernel, out_shape=pltpu.HBM((20 * L, L), BF16), i...  5.31 us
    all_to_all x1, starting transfers between devices, body(): grads = lax.all_to_all(spread, 'tp', 0, 0, tiled=True)  4.02 us
  transfers between devices with their start and end apart: 4, of which 4 were waited for; matrix products, arithmetic and copies ran while one was open for 0% of the time, Pallas kernels for 5%

profile of v4, /device:TPU:25, one launch (start us, length us, event | category | flops | bytes accessed | tf_op | source)
XLA Modules:
  0.0 122.1 jit_solution(13016360437645564283)
XLA Ops:
  0.6 1.7 %spread.1 = bf16[4,128,512]{2,1,0:T(8,128)(2,1)} custom-call(bf16[128,512]{1,0:T(8,128)(2,1)} %grads.1), custom_call_target="tpu_custom_call" | custom-call | tf_op jit(solution)/shard_map/spread/pallas_call | solution.py:329
  2.4 4.0 %all-to-all-start = ((bf16[4,128,512]{2,1,0:T(8,128)(2,1)}), bf16[4,128,512]{2,1,0:T(8,128)(2,1)S(1)}, u32[]{:S(2)}, u32[]{:S(2)}) async-start(bf16[4,128,512]{2,1,0:T(8,128)(2,1)} %spread.1), calls=%async_computation | async-start | bytes 1048576 | tf_op jit(solution)/shard_map/all_to_all | solution.py:338
  6.4 2.4 %stage.1 = (bf16[128,16,128]{2,1,0:T(8,128)(2,1)}, bf16[128,8,128]{2,1,0:T(8,128)(2,1)S(1)}, bf16[128,512]{1,0:T(8,128)(2,1)S(1)}, bf16[512,128]{1,0:T(8,128)(2,1)S(1)}, bf16[512,2048]{1,0:T(8,128)(2,1)S(1)}) custom-call(bf16[128,512]{1,0:T(8,128)(2,1)} %lf.1, bf16[128,512]{1,0:T(8,128)(2,1)} %sk.3, bf16[128,512]{1,0:T(8,128)(2,1)} %sv.3, ...), custom_call_target="tpu_custom_call" | custom-call | tf_op jit(solution)/shard_map/stage/pallas_call | solution.py:342
  8.8 5.9 %all-to-all-done.grads = bf16[4,128,512]{2,1,0:T(8,128)(2,1)S(1)} async-done(((bf16[4,128,512]{2,1,0:T(8,128)(2,1)}), bf16[4,128,512]{2,1,0:T(8,128)(2,1)S(1)}, u32[]{:S(2)}, u32[]{:S(2)}) %all-to-all-start) | async-done | bytes 524320 | tf_op jit(solution)/shard_map/all_to_all | solution.py:338
  14.7 0.0 copy-start
  14.7 1.5 %join.1 = (bf16[128,16,128]{2,1,0:T(8,128)(2,1)}, bf16[512,128]{1,0:T(8,128)(2,1)S(1)}) custom-call(bf16[4,128,512]{2,1,0:T(8,128)(2,1)S(1)} %all-to-all-done.grads, bf16[128,8,128]{2,1,0:T(8,128)(2,1)S(1)} %get-tuple-element.21.gate, bf16[512,2048]{1,0:T(8,128)(2,1)S(1)} %get-tuple-element.22.weight, ...), custom_call_target="tpu_custom_call", output_to_operand_aliasing={{0}: (4, {})} | custom-call | tf_op jit(solution)/shard_map/join/pallas_call | solution.py:354
  16.2 21.0 %all-to-all-start.1 = ((bf16[128,16,128]{2,1,0:T(8,128)(2,1)}), bf16[128,16,128]{2,1,0:T(8,128)(2,1)S(1)}, u32[]{:S(2)}, u32[]{:S(2)}) async-start(bf16[128,16,128]{2,1,0:T(8,128)(2,1)} %get-tuple-element.25), calls=%async_computation.1 | async-start | bytes 1048576 | tf_op jit(solution)/shard_map/all_to_all | solution.py:366
  37.2 1.2 load.1
  38.4 0.0 copy-start.1
  38.4 0.0 copy-start.2
  38.4 0.0 copy-start.3
  38.4 0.0 copy-start.4
  38.5 31.5 %all-to-all-done.1.arrived = bf16[128,16,128]{2,1,0:T(8,128)(2,1)S(1)} async-done(((bf16[128,16,128]{2,1,0:T(8,128)(2,1)}), bf16[128,16,128]{2,1,0:T(8,128)(2,1)S(1)}, u32[]{:S(2)}, u32[]{:S(2)}) %all-to-all-start.1) | async-done | bytes 524320 | tf_op jit(solution)/shard_map/all_to_all | solution.py:366
  69.9 0.0 copy-done
  70.0 5.3 %spectral.1 = bf16[2560,128]{1,0:T(8,128)(2,1)} custom-call(s32[1]{0:T(128)} %bitcast.place, bf16[128,16,128]{2,1,0:T(8,128)(2,1)S(1)} %all-to-all-done.1.arrived, bf16[128,512]{1,0:T(8,128)(2,1)S(1)} %copy-done, bf16[256,256]{1,0:T(8,128)(2,1)S(1)} %get-tuple-element.26.forward, bf16[256,256]{1,0:T(8,128)(2,1)S(1)} %get-tuple-element.27.high_ref, ...), custom_call_target="tpu_custom_call" | custom-call | tf_op jit(solution)/shard_map/spectral/pallas_call | solution.py:388
  75.3 7.2 %all-to-all-start.2 = ((bf16[128,5,4,128]{3,2,1,0:T(4,128)(2,1)}), bf16[128,5,4,128]{3,2,1,0:T(4,128)(2,1)S(1)}, u32[]{:S(2)}, u32[]{:S(2)}) async-start(bf16[128,5,4,128]{3,2,1,0:T(4,128)(2,1)} %bitcast.4), calls=%async_computation.2 | async-start | bytes 1310720 | tf_op jit(solution)/shard_map/all_to_all | solution.py:401
  82.5 3.4 %collective-permute-start = (bf16[128,512]{1,0:T(8,128)(2,1)S(1)}, bf16[128,512]{1,0:T(8,128)(2,1)S(1)}, u32[]{:S(2)}, u32[]{:S(2)}) collective-permute-start(bf16[128,512]{1,0:T(8,128)(2,1)S(1)} %get-tuple-element.34.prod), channel_id=1, source_target_pairs={{0,4},{4,8},{8,12},{12,16},{16,20},{20,24},{24,28},{28,32},{32,36}... | collective-permute-start | bytes 393224 | tf_op jit(solution)/shard_map/ppermute | solution.py:320
  85.8 22.3 %collective-permute-done.before = bf16[128,512]{1,0:T(8,128)(2,1)S(1)} collective-permute-done((bf16[128,512]{1,0:T(8,128)(2,1)S(1)}, bf16[128,512]{1,0:T(8,128)(2,1)S(1)}, u32[]{:S(2)}, u32[]{:S(2)}) %collective-permute-start) | collective-permute-done | bytes 131104 | tf_op jit(solution)/shard_map/ppermute | solution.py:320
  108.1 2.7 %mix.1.short_mix = f32[128,512]{1,0:T(8,128)S(1)} custom-call(bf16[128,512]{1,0:T(8,128)(2,1)S(1)} %collective-permute-done.before, bf16[128,512]{1,0:T(8,128)(2,1)S(1)} %get-tuple-element.34.prod, bf16[128,512]{1,0:T(8,128)(2,1)S(1)} %copy-done), custom_call_target="tpu_custom_call" | custom-call | tf_op jit(solution)/shard_map/mix/pallas_call | solution.py:380
  110.8 9.9 %all-to-all-done.2 = bf16[128,5,4,128]{3,2,1,0:T(4,128)(2,1)S(1)} async-done(((bf16[128,5,4,128]{3,2,1,0:T(4,128)(2,1)}), bf16[128,5,4,128]{3,2,1,0:T(4,128)(2,1)S(1)}, u32[]{:S(2)}, u32[]{:S(2)}) %all-to-all-start.2) | async-done | bytes 655392 | tf_op jit(solution)/shard_map/all_to_all | solution.py:401
  120.7 0.0 copy-done.1
  120.7 0.0 copy-done.2
  120.7 0.0 copy-done.3
  120.7 0.0 copy-done.4
  120.7 1.4 %post.1 = (bf16[128,512]{1,0:T(8,128)(2,1)}, bf16[128,512]{1,0:T(8,128)(2,1)}, bf16[128,512]{1,0:T(8,128)(2,1)}, bf16[128,512]{1,0:T(8,128)(2,1)}, bf16[128,512]...) custom-call(bf16[2560,128]{1,0:T(8,128)(2,1)S(1)} %bitcast.3, ...), custom_call_target="tpu_custom_call" | custom-call | tf_op jit(solution)/shard_map/post/pallas_call | solution.py:402
Async XLA Ops:
  2.4 12.4 %all-to-all-start = ((bf16[4,128,512]{2,1,0:T(8,128)(2,1)}), bf16[4,128,512]{2,1,0:T(8,128)(2,1)S(1)}, u32[]{:S(2)}, u32[]{:S(2)}) async-start(bf16[4,128,512]{2,1,0:T(8,128)(2,1)} %spread.1), calls=%async_computation | async-start | bytes 1048576 | tf_op jit(solution)/shard_map/all_to_all | solution.py:338
  14.7 55.2 %copy-start = (bf16[128,512]{1,0:T(8,128)(2,1)S(1)}, bf16[128,512]{1,0:T(8,128)(2,1)}, u32[]{:S(2)}) copy-start(bf16[128,512]{1,0:T(8,128)(2,1)} %taps_in.3) | copy-start | bytes 393220
  16.2 53.7 %all-to-all-start.1 = ((bf16[128,16,128]{2,1,0:T(8,128)(2,1)}), bf16[128,16,128]{2,1,0:T(8,128)(2,1)S(1)}, u32[]{:S(2)}, u32[]{:S(2)}) async-start(bf16[128,16,128]{2,1,0:T(8,128)(2,1)} %get-tuple-element.25), calls=%async_computation.1 | async-start | bytes 1048576 | tf_op jit(solution)/shard_map/all_to_all | solution.py:366
  38.4 82.3 %copy-start.1 = (bf16[128,512]{1,0:T(8,128)(2,1)S(1)}, bf16[128,512]{1,0:T(8,128)(2,1)}, u32[]{:S(2)}) copy-start(bf16[128,512]{1,0:T(8,128)(2,1)} %sk.3) | copy-start | bytes 393220
  38.4 82.2 %copy-start.2 = (bf16[128,512]{1,0:T(8,128)(2,1)S(1)}, bf16[128,512]{1,0:T(8,128)(2,1)}, u32[]{:S(2)}) copy-start(bf16[128,512]{1,0:T(8,128)(2,1)} %sv.3) | copy-start | bytes 393220
  38.4 82.2 %copy-start.3 = (bf16[128,512]{1,0:T(8,128)(2,1)S(1)}, bf16[128,512]{1,0:T(8,128)(2,1)}, u32[]{:S(2)}) copy-start(bf16[128,512]{1,0:T(8,128)(2,1)} %lk.3) | copy-start | bytes 393220
  38.4 82.2 %copy-start.4 = (bf16[128,512]{1,0:T(8,128)(2,1)S(1)}, bf16[128,512]{1,0:T(8,128)(2,1)}, u32[]{:S(2)}) copy-start(bf16[128,512]{1,0:T(8,128)(2,1)} %sq.3) | copy-start | bytes 393220
  75.3 45.4 %all-to-all-start.2 = ((bf16[128,5,4,128]{3,2,1,0:T(4,128)(2,1)}), bf16[128,5,4,128]{3,2,1,0:T(4,128)(2,1)S(1)}, u32[]{:S(2)}, u32[]{:S(2)}) async-start(bf16[128,5,4,128]{3,2,1,0:T(4,128)(2,1)} %bitcast.4), calls=%async_computation.2 | async-start | bytes 1310720 | tf_op jit(solution)/shard_map/all_to_all | solution.py:401
  82.5 25.7 %collective-permute-start = (bf16[128,512]{1,0:T(8,128)(2,1)S(1)}, bf16[128,512]{1,0:T(8,128)(2,1)S(1)}, u32[]{:S(2)}, u32[]{:S(2)}) collective-permute-start(bf16[128,512]{1,0:T(8,128)(2,1)S(1)} %get-tuple-element.34.prod), channel_id=1, source_target_pairs={{0,4},{4,8},{8,12},{12,16},{16,20},{20,24},{24,28},{28,32},{32,36}... | collective-permute-start | bytes 393224 | tf_op jit(solution)/shard_map/ppermute | solution.py:320
